TPU v7x, 256 devices: a whole 4x4x8 slice. The times are simulated.
256 devices in a mesh: sample: 8 (over y_lo, x), seq: 16 (over y_hi, z), head: 2 (over core).
Axes of the slice: x: 4, y: 4 (y_hi: 2, y_lo: 2; y = y_hi * 2 + y_lo), z: 8, core: 2. Of those that a mesh axis runs over, the one named last changes fastest.
Arguments:
- values: bfloat16 [8, 8192, 4096], P('sample', 'seq', 'head'), may hold values from -6 to 6
- gate_values: bfloat16 [8, 8192, 4096], P('sample', 'seq', 'head'), may hold values from -6 to 6
- state_in: bfloat16 [8, 8192, 128], P('sample', 'seq'), may hold values from -0.5 to 0.5
- state_out: bfloat16 [8, 8192, 128], P('sample', 'seq'), may hold values from -0.5 to 0.5
- step_size: float32 [8, 8192, 64], P('sample', 'seq', 'head'), may hold values from 0.25 to 1
- log_decay: float32 [8, 8192, 64], P('sample', 'seq', 'head'), may hold values from -1 to 0, as said below
- skip_gain: float32 [64], P('head'), may hold values from 0.5 to 1.5
- norm_gain: float32 [4096], P('head'), may hold values from 0.25 to 1.75
- out_weight: bfloat16 [4096, 4096], P('head', 'seq'), may hold values from -0.09375 to 0.09375
- prompt_state: float32 [64, 64, 128], P('head', None, 'sample'), may hold values from -16 to 16
Outputs:
- projected: bfloat16 [8, 8192, 4096], P('sample', 'seq', 'head')
Inputs may be any that keep to these rules, and one draw needn't show every extreme that they name: `log_decay`: every entry is negative.
All inputs are finite; a program needn't handle non-finite values.
Results may differ from a plain program's by a relative error of at most 0.019.
Values may be sent and summed in bfloat16 or wider, within the bound.
A program may use at most 128 MiB of HBM per device.

v0:
```python
from functools import partial

import jax
import jax.numpy as jnp
from jax import lax
from jax.sharding import Mesh
from jax.sharding import PartitionSpec as P

P_SIZE = 64
L = 256
GROUP_HEADS = 8
SEQ = ("seq_0", "seq_1")


EPSILON = 1e-05


def neutral_like(array, identity):
    return jax.tree.map(
        lambda a, e: jnp.broadcast_to(jnp.asarray(e, a.dtype), a.shape), array, identity
    )


def entering(array, axes, combine, identity):
    before = start = neutral_like(array, identity)
    so_far = array
    for axis in reversed(axes):
        peers, index = (lax.axis_size(axis), lax.axis_index(axis))
        pieces = jax.tree.map(
            lambda part, kind: lax.all_gather(part.astype(kind), axis),
            so_far,
            (jnp.bfloat16, jnp.bfloat16),
        )
        inside, so_far = (start, start)
        for k in range(peers):
            passed = k < index
            so_far = combine(
                so_far, jax.tree.map(lambda part, own: part[k].astype(own.dtype), pieces, array)
            )
            inside = jax.tree.map(lambda new, old: jnp.where(passed, new, old), so_far, inside)
        before = combine(inside, before)
    return before


def in_blocks(array, dim, peers):
    dims = array.shape
    tiles = array.reshape(*dims[:dim], peers, dims[dim] // peers, *dims[dim + 1 :])
    return jnp.moveaxis(tiles, dim, 0)


def sent_and_summed(array, axis, dim):
    peers = lax.axis_size(axis)
    tiles = lax.all_to_all(in_blocks(array, dim, peers), axis, 0, 0, tiled=True)
    return jnp.sum(tiles.astype(jnp.float32), axis=0)


def block_terms(values_blk, in_blk, out_blk, step_blk, decay_blk, skip_gain):
    heads = decay_blk.shape[1]
    running = jnp.cumsum(decay_blk, axis=0)
    per_head = values_blk.reshape(values_blk.shape[0], heads, -1)
    scaled = (per_head.astype(jnp.float32) * step_blk[:, :, None]).astype(jnp.bfloat16)
    scores = jnp.dot(out_blk, in_blk.T, preferred_element_type=jnp.float32)
    token_offset = jnp.arange(values_blk.shape[0])
    causal = token_offset[:, None] >= token_offset[None, :]
    by_head = running.T
    spread = by_head[:, :, None] - by_head[:, None, :]
    pair_decay = jnp.exp(jnp.where(causal[None], spread, -1e30))
    mixing = (scores[None] * pair_decay).astype(jnp.bfloat16)
    inner = jnp.einsum("hts,shp->thp", mixing, scaled, preferred_element_type=jnp.float32)
    tail = jnp.exp(running[-1][None, :] - running)
    weighted = (scaled.astype(jnp.float32) * tail[:, :, None]).astype(jnp.bfloat16)
    block_state = jnp.einsum("shp,sn->hpn", weighted, in_blk, preferred_element_type=jnp.float32)
    local_out = inner + skip_gain[None, :, None] * per_head.astype(jnp.float32)
    return (local_out, running, block_state)


def local_sweep(values_s, in_s, out_s, step_s, decay_s, skip_gain):
    count = values_s.shape[0] // L
    heads = decay_s.shape[1]
    width = values_s.shape[1] // heads
    states = in_s.shape[1]
    blocks = (
        values_s.reshape(count, L, -1),
        in_s.reshape(count, L, -1),
        out_s.reshape(count, L, -1),
        step_s.reshape(count, L, heads),
        decay_s.reshape(count, L, heads),
    )

    def advance(carry, block):
        state, total = carry
        values_blk, in_blk, out_blk, step_blk, decay_blk = block
        local_out, running, block_state = block_terms(
            values_blk, in_blk, out_blk, step_blk, decay_blk, skip_gain
        )
        new_state = jnp.exp(running[-1])[:, None, None] * state + block_state
        return ((new_state, total + running[-1]), (local_out, running, state, total))

    initial = (jnp.zeros((heads, width, states), jnp.float32), jnp.zeros((heads,), jnp.float32))
    return lax.scan(advance, initial, blocks)


def link(earlier, later):
    decay_early, state_early = earlier
    decay_late, state_late = later
    return (decay_early * decay_late, decay_late[:, :, None, None] * state_early + state_late)


def group_norm(gated, norm_gain):
    width = GROUP_HEADS * P_SIZE
    grouped = gated.reshape(gated.shape[0], -1, width)
    mean_square = jnp.mean(grouped * grouped, axis=-1, keepdims=True)
    rescaled = grouped * lax.rsqrt(mean_square + EPSILON)
    return (rescaled.reshape(gated.shape) * norm_gain).astype(jnp.bfloat16)


def shards(
    values,
    gate_values,
    state_in,
    state_out,
    step_size,
    log_decay,
    skip_gain,
    norm_gain,
    out_weight,
    prompt_state,
):
    prompt = lax.all_gather(prompt_state.astype(jnp.bfloat16), "sample", axis=2, tiled=True).astype(
        prompt_state.dtype
    )
    sweep_sample = partial(local_sweep, skip_gain=skip_gain)
    (last_state, last_total), (local_out, running, before, totals) = jax.vmap(sweep_sample)(
        values, state_in, state_out, step_size, log_decay
    )
    identity = (jnp.ones_like(last_total), jnp.zeros_like(last_state))
    lead_decay, lead_state = entering((jnp.exp(last_total), last_state), SEQ, link, identity)
    entry = lead_state + lead_decay[:, :, None, None] * prompt[None]
    start = before + jnp.exp(totals)[:, :, :, None, None] * entry[:, None]
    start_low = start.astype(jnp.bfloat16)
    samples, tokens = (values.shape[0], values.shape[1])
    count = tokens // L
    out_blocks = state_out.reshape(samples, count, L, -1)
    carried = jnp.exp(running)[..., None] * jnp.einsum(
        "sktn,skhpn->skthp", out_blocks, start_low, preferred_element_type=jnp.float32
    )
    outputs = (local_out + carried).reshape(samples * tokens, -1)
    gated = outputs * jax.nn.silu(gate_values.reshape(samples * tokens, -1).astype(jnp.float32))
    normed = group_norm(gated, norm_gain)
    terms = jnp.dot(
        normed,
        lax.all_gather(out_weight, SEQ, axis=1, tiled=True),
        preferred_element_type=jnp.float32,
    )
    mine = sent_and_summed(terms.astype(jnp.bfloat16), "head", 1).astype(jnp.bfloat16)
    return mine.reshape(samples, tokens, -1)


def solution(mesh):
    split = Mesh(
        mesh.devices.reshape(mesh.shape["sample"], 2, 8, mesh.shape["head"]),
        ("sample", "seq_0", "seq_1", "head"),
    )
    return jax.shard_map(
        shards,
        mesh=split,
        in_specs=(
            P("sample", SEQ, "head"),
            P("sample", SEQ, "head"),
            P("sample", SEQ, None),
            P("sample", SEQ, None),
            P("sample", SEQ, "head"),
            P("sample", SEQ, "head"),
            P("head"),
            P("head"),
            P("head", SEQ),
            P("head", None, "sample"),
        ),
        out_specs=P("sample", SEQ, "head"),
        check_vma=False,
    )
```

profile of v0, /device:TPU:1, one launch (start us, length us, event | category | flops | bytes accessed | tf_op | source)
XLA Modules:
  0.0 401.1 jit_solution(16443783522025192746)
XLA Ops:
  6.5 0.9 reshape.580
  7.4 0.9 reshape.582
  8.3 22.3 %while.21 = (s32[]{:T(128)}, f32[1,32,64,128]{3,2,1,0:T(8,128)S(1)}, f32[1,32]{1,0:T(1,128)S(1)}, f32[2,1,256,32,64]{2,4,3,1,0:T(8,128)}, f32[2,1,256,32]{2,0,3,...) while((s32[]{:T(128)}, ...), condition=%wide.region_3.4_spmd.clone, body=%wide.region_0.3_spmd.clone.sunk | while | flops 435765440 | bytes 33923384 | solution.py:100
  8.5 0.6 reduce-window.14
  9.6 1.3 constant_dynamic-slice_fusion.6
  10.9 0.5 copy.90
  11.6 0.2 fusion.101
  11.8 3.7 fusion.102
  15.6 0.5 slice_reduce_fusion.5
  16.2 0.2 mul.830
  16.4 0.2 mul.831
  16.6 0.5 multiply_convert_fusion.13
  17.1 1.0 bitcast_dynamic-update-slice_fusion.2
  18.1 0.5 fusion.100
  18.7 0.2 dynamic_update_slice.30
  18.8 0.6 copy-done.10
  19.6 0.6 reduce-window.14
  20.7 1.3 constant_dynamic-slice_fusion.6
  22.0 0.5 copy.90
  22.7 0.2 fusion.101
  22.9 3.8 fusion.102
  26.8 0.5 slice_reduce_fusion.5
  27.4 0.2 mul.830
  27.7 0.5 multiply_convert_fusion.13
  28.3 1.0 bitcast_dynamic-update-slice_fusion.2
  29.3 0.5 fusion.100
  29.8 0.2 dynamic_update_slice.30
  30.0 0.6 copy-done.10
  30.6 0.9 convert_element_type.469
  31.6 16.1 %all-gather.2 = bf16[8,1,32]{2,1,0:T(2,128)(2,1)S(1)} all-gather(bf16[1,1,32]{2,1,0:T(2,128)(2,1)S(1)} %convert_bitcast_fusion.16), channel_id=2, replica_groups=mesh['sample'=8,'seq_0'=2,'seq_1'=8,'head'=2] {'seq_1'}, dimensions={0}, use_global_device_ids=true | all-gather | bytes 576 | tf_op jit(solution)/shard_map/all_gather | solution.py:30
  47.7 42.6 %all-gather.11.cloned.1.call-done = bf16[8,32,64,128]{3,2,1,0:T(8,128)(2,1)} async-done(((bf16[1,32,64,128]{3,2,1,0:T(8,128)(2,1)}), bf16[8,32,64,128]{3,2,1,0:T(8,128)(2,1)}) %all-gather.11.cloned.1.call-update) | async-done | bytes 4194320 | tf_op jit(solution)/shard_map/all_gather | solution.py:30
  90.3 3.5 fusion.70
  93.8 0.7 all-gather.9.cloned.1.call-update
  94.5 4.6 %all_gather.28 = bf16[2,1,32]{2,1,0:T(2,128)(2,1)S(1)} all-gather(bf16[1,1,32]{2,1,0:T(2,128)(2,1)S(1)} %fusion.76), channel_id=1, replica_groups=mesh['sample'=8,'seq_0'=2,'seq_1'=8,'head'=2] {'seq_0'}, dimensions={0}, use_global_device_ids=true | all-gather | bytes 192 | tf_op jit(solution)/shard_map/all_gather | solution.py:30
  99.2 25.5 %all_gather.32 = bf16[32,64,128]{1,0,2:T(8,128)(2,1)S(1)} all-gather(bf16[32,64,16]{1,0,2:T(8,128)(2,1)S(1)} %copy.70), channel_id=1, replica_groups=mesh['sample'=8,'seq_0'=2,'seq_1'=8,'head'=2] {'sample'}, dimensions={2}, use_global_device_ids=true | all-gather | bytes 589824 | tf_op jit(solution)/shard_map/all_gather | solution.py:129
  124.8 1.1 copy.48
  126.0 2.9 copy.50
  128.8 4.0 %reshape.612 = f32[2,256,32,64]{1,0,3,2:T(2,128)} reshape(bf16[1,512,2048]{1,2,0:T(8,128)(2,1)S(1)} %copy.50) | data formatting | bytes 6291456 | tf_op jit(solution)/shard_map/convert_element_type | solution.py:148
  132.9 4.9 %fusion.55 = f32[32,64,128]{2,1,0:T(8,128)S(1)} fusion(bf16[32,64,128]{2,1,0:T(8,128)(2,1)S(1)} %copy.48, bf16[2,1,32,64,128]{4,3,2,1,0:T(8,128)(2,1)} %all-gather.7.cloned.1.call-done, f32[32]{0:T(128)S(1)} %get-tuple-element.190, f32[32]{0:T(128)S(1)} %bitcast_multiply_fusion.6, f32[32]{0:T(128)S(1)} %get-tuple-element.197, f32[32]{0:T(128)S(1)} %get-tuple-element.202, ...), kind=kLoop, calls=%fused_computation.102 | loop fusion | flops 11272192 | bytes 6817290 | tf_op jit(solution)/shard_map/add | solution.py:138
  137.9 3.6 multiply_reduce_fusion
  141.5 3.4 copy.49
  144.9 2.4 copy.62
  147.5 4.0 fusion.21
  151.5 213.7 %all-gather.9.cloned.1.call-done = bf16[2048,4096]{1,0:T(8,128)(2,1)} async-done(((bf16[2048,256]{1,0:T(8,128)(2,1)}), bf16[2048,4096]{1,0:T(8,128)(2,1)}) %all-gather.9.cloned.1.call-update) | async-done | bytes 16777232 | tf_op jit(solution)/shard_map/all_gather | solution.py:152
  365.2 13.2 %convolution_convert_fusion = bf16[512,4096]{1,0:T(8,128)(2,1)S(1)} fusion(bf16[512,2048]{0,1:T(8,128)(2,1)} %fusion.21, bf16[2048,4096]{1,0:T(8,128)(2,1)} %all-gather.9.cloned.1.call-done), kind=kOutput, calls=%fused_computation.43 | convolution fusion | flops 8592031744 | bytes 23068672 | tf_op jit(solution)/shard_map/dot_general | solution.py:150
  378.3 0.3 copy.73
  378.7 10.8 %all_to_all.5 = bf16[2,512,2048]{2,1,0:T(8,128)(2,1)} all-to-all(bf16[2,512,2048]{2,1,0:T(8,128)(2,1)S(1)} %bitcast.450), channel_id=1, replica_groups=mesh['sample'=8,'seq_0'=2,'seq_1'=8,'head'=2] {'head'}, dimensions={0} | all-to-all | bytes 8388608 | tf_op jit(solution)/shard_map/all_to_all | solution.py:53
  389.5 5.1 %reduce_sum.31 = bf16[512,2048]{1,0:T(8,128)(2,1)} reduce(bf16[2,512,2048]{2,1,0:T(8,128)(2,1)} %all_to_all.5, bf16[]{:T(256)} %constant.71.clone.1), dimensions={0}, to_apply=%region_6.7 | reduce | flops 1048576 | bytes 6291458 | tf_op jit(solution)/shard_map/reduce_sum | solution.py:54
  (112 shorter events, 2.6 us)
Async XLA Ops:
  6.5 83.8 %all-gather.11.cloned.1.call-start = ((), (), s32[]{:S(2)}) async-start(), calls=%async_computation.3 | async-start | bytes 4718592 | tf_op jit(solution)/shard_map/all_gather | solution.py:30
  8.3 1.2 copy-start.4
  8.3 1.2 copy-start.6
  8.3 3.2 copy-start.1
  8.4 3.2 copy-start.2
  8.4 3.4 copy-start.14
  17.0 1.6 copy-start.9
  17.1 2.4 copy-start.5
  17.1 2.4 copy-start.7
  18.8 0.6 copy-start.10
  19.4 1.2 copy-start.4
  19.4 1.2 copy-start.6
  19.4 3.2 copy-start.1
  19.5 3.2 copy-start.2
  19.5 3.4 copy-start.14
  28.2 1.6 copy-start.9
  28.2 2.4 copy-start.5
  28.2 2.4 copy-start.7
  30.0 0.6 copy-start.10
  30.6 68.5 %copy-start.8 = (f32[32,64,16]{1,2,0:T(8,128)S(1)}, f32[32,64,16]{1,2,0:T(8,128)}, u32[]{:S(2)}) copy-start(f32[32,64,16]{1,2,0:T(8,128)} %param.21) | copy-start | bytes 393220
  31.5 101.4 %all-gather.7.cloned.1.call-start = ((), (), s32[]{:S(2)}) async-start(), calls=%async_computation.1 | async-start | bytes 1572864 | tf_op jit(solution)/shard_map/all_gather | solution.py:30
  90.3 35.6 %copy-start.11 = (f32[2,1,256,32]{2,0,3,1:T(2,128)S(1)}, f32[2,1,256,32]{2,0,3,1:T(2,128)}, u32[]{:S(2)}) copy-start(f32[2,1,256,32]{2,0,3,1:T(2,128)} %get-tuple-element.78) | copy-start | bytes 196612
  93.8 271.4 %all-gather.9.cloned.1.call-start = ((), (), s32[]{:S(2)}) async-start(), calls=%async_computation.2 | async-start | bytes 17825792 | tf_op jit(solution)/shard_map/all_gather | solution.py:152
  132.8 5.0 %copy-start.3 = (bf16[2,1,256,128]{3,2,1,0:T(8,128)(2,1)S(1)}, bf16[2,1,256,128]{3,2,1,0:T(8,128)(2,1)}, u32[]{:S(2)}) copy-start(bf16[2,1,256,128]{3,2,1,0:T(8,128)(2,1)} %get-tuple-element.351) | copy-start | bytes 393220
  132.9 4.9 %copy-start = (f32[2,256,32,64]{1,0,3,2:T(2,128)S(1)}, f32[2,256,32,64]{1,0,3,2:T(2,128)}, u32[]{:S(2)}) copy-start(f32[2,256,32,64]{1,0,3,2:T(2,128)} %reshape.612) | copy-start | bytes 12582916
  132.9 4.9 %copy-start.13 = (f32[2,1,32,64,128]{4,3,2,1,0:T(8,128)S(1)}, f32[2,1,32,64,128]{4,3,2,1,0:T(8,128)}, u32[]{:S(2)}) copy-start(f32[2,1,32,64,128]{4,3,2,1,0:T(8,128)} %get-tuple-element.79) | copy-start | bytes 6291460
  144.9 2.6 copy-start.12
Sparse Core Ops, SparseCore 0:
  31.6 58.6 all-gather.10
  93.9 34.4 all-gather.6
  130.9 234.2 all-gather.8
where the time goes:
time: 402 us; the launch traced here: 401 us
  waiting for transfers between devices  257 us (64%)
  blocking collectives  57.1 us (14%)
  matrix products  25.6 us (6%)
  local copies, waits for them, and re-layouts  23.9 us (6%)
  other arithmetic  23.5 us (6%)
  between operations  13.3 us (3%)
    all_gather x1, waiting for transfers between devices, shards(): lax.all_gather(out_weight, SEQ, axis=1, tiled=True)  214 us
    all_gather x2, waiting for transfers between devices, entering(): lax.all_gather(part.astype(kind), axis)  42.6 us
    all_gather x1, blocking collectives, shards(): lax.all_gather(prompt_state.astype(jnp.bfloat16), 'sample', axis=2, tiled...  25.5 us
    all_gather x2, blocking collectives, entering(): lax.all_gather(part.astype(kind), axis)  20.7 us
    dot_general x1, matrix products, shards(): jnp.dot(normed, lax.all_gather(out_weight, SEQ, axis=1, tiled=True), pref...  13.2 us
    all_to_all x1, blocking collectives, sent_and_summed(): tiles = lax.all_to_all(in_blocks(array, dim, peers), axis, 0, 0, tiled=True)  10.8 us
  transfers between devices with their start and end apart: 3, of which 2 were waited for; matrix products, arithmetic and copies ran while one was open for 7% of the time, Pallas kernels for 0%

commit v1 on v0

--- a/solution.py
+++ b/solution.py
@@ -3,16 +3,299 @@
 import jax
 import jax.numpy as jnp
 from jax import lax
+from jax.experimental import pallas as pl
+from jax.experimental.pallas import tpu as pltpu
 from jax.sharding import Mesh
 from jax.sharding import PartitionSpec as P
 
 P_SIZE = 64
 L = 256
 GROUP_HEADS = 8
-SEQ = ("seq_0", "seq_1")
-
-
+SEQ = ("yhi", "z")
+SAMPLE = ("ylo", "x")
+NZ = 8
+MESH_ID = pl.DeviceIdType.MESH
 EPSILON = 1e-05
+
+
+def place():
+    names = ("ylo", "x", "yhi", "z", "head")
+    at = {name: lax.axis_index(name) for name in names}
+    y = at["yhi"] * 2 + at["ylo"]
+    up, down = lax.rem(y + 1, 4), lax.rem(y + 3, 4)
+    near = {
+        "+x": {"x": lax.rem(at["x"] + 1, 4)},
+        "-x": {"x": lax.rem(at["x"] + 3, 4)},
+        "+y": {"yhi": up // 2, "ylo": lax.rem(up, 2)},
+        "-y": {"yhi": down // 2, "ylo": lax.rem(down, 2)},
+        "+z": {"z": lax.rem(at["z"] + 1, NZ)},
+        "-z": {"z": lax.rem(at["z"] + NZ - 1, NZ)},
+        "across": {"yhi": 1 - at["yhi"], "ylo": 1 - at["ylo"]},
+        "sibling": {"head": 1 - at["head"]},
+    }
+    return at, near
+
+
+WAYS = ("+x", "-x", "+y", "-y")
+
+
+class Gather:
+    def __init__(self, at, near, own, wbuf, sems):
+        self.at, self.near, self.own, self.wbuf = at, near, own, wbuf
+        self.zs, self.zr, self.fs, self.fr, self.gs, self.gr, self.ls = sems
+        px, lo = lax.rem(at["x"], 2), at["ylo"]
+        self.mine = px * 2 + lo
+        self.byx = (1 - px) * 2 + lo
+        self.byy = px * 2 + 1 - lo
+        self.px = px
+        self.s_own = at["yhi"] * NZ + at["z"]
+        self.s_across = (1 - at["yhi"]) * NZ + at["z"]
+
+    def copy(self, src, s, start, size, send, recv, to):
+        dst = self.wbuf.at[s, pl.ds(start, size)]
+        return pltpu.make_async_remote_copy(
+            src_ref=dst if src is None else src,
+            dst_ref=dst,
+            send_sem=send,
+            recv_sem=recv,
+            device_id=self.near[to],
+            device_id_type=MESH_ID,
+        )
+
+    def shard(self, fam, z):
+        hi = self.at["yhi"] if fam == 0 else 1 - self.at["yhi"]
+        return hi * NZ + lax.rem(z + 2 * NZ, NZ)
+
+    def events(self, n):
+        fam, k = n % 2, n // 2
+        found = []
+        if k < (4 if fam == 0 else 3):
+            found.append((self.shard(fam, self.at["z"] - 1 - k), k, "+z"))
+        if k < (3 if fam == 0 else 4):
+            found.append((self.shard(fam, self.at["z"] + 1 + k), k, "-z"))
+        return fam, found
+
+    def ring(self, s, way, slot, src=None):
+        return self.copy(src, s, self.mine * 4, 4, self.zs.at[slot], self.zr.at[s], way)
+
+    def local(self):
+        return pltpu.make_async_copy(self.own, self.wbuf.at[self.s_own], self.ls)
+
+    def give(self):
+        start = self.px * 8
+        src = self.own.at[pl.ds(start, 8)]
+        return self.copy(src, self.s_own, start, 8, self.zs.at[0], self.zr.at[self.s_own], "across")
+
+    def given(self):
+        start = self.px * 8
+        return self.copy(None, self.s_across, start, 8, self.zs.at[0], self.zr.at[self.s_across], "across")
+
+    def give_on(self, d):
+        start = self.px * 8 + 4 * d
+        return self.copy(
+            None, self.s_across, start, 4, self.fs.at[0, d], self.fr.at[self.s_across, d], WAYS[d]
+        )
+
+    def given_on(self, d):
+        start = (1 - self.px) * 8 + 4 * d
+        return self.copy(
+            None, self.s_across, start, 4, self.fs.at[0, d], self.fr.at[self.s_across, d], WAYS[d]
+        )
+
+    def first(self, s, d, slot):
+        start = self.mine * 4 + 2 * (d % 2)
+        return self.copy(None, s, start, 2, self.fs.at[slot, d], self.fr.at[s, d], WAYS[d])
+
+    def first_in(self, s, d):
+        start = (self.byx if d < 2 else self.byy) * 4 + 2 * (d % 2)
+        return self.copy(None, s, start, 2, self.fs.at[0, d], self.fr.at[s, d], WAYS[d])
+
+    def second(self, s, d, slot):
+        start = (self.byy if d < 2 else self.byx) * 4 + (0, 2, 1, 3)[d]
+        return self.copy(None, s, start, 1, self.gs.at[slot, d], self.gr.at[s, d], WAYS[d])
+
+    def second_in(self, s, d):
+        far = 3 - self.mine
+        start = far * 4 + (0, 2, 1, 3)[d]
+        return self.copy(None, s, start, 1, self.gs.at[0, d], self.gr.at[s, d], WAYS[d])
+
+    def begin(self):
+        src = self.own.at[pl.ds(self.mine * 4, 4)]
+        self.sent = []
+        for c in (
+            self.ring(self.s_own, "+z", 1, src),
+            self.ring(self.s_own, "-z", 2, src),
+            self.give(),
+        ):
+            c.start()
+            self.sent.append(c)
+        self.local().start()
+        self.slots = {"z": 3, "f": 1, "g": 0}
+
+    def begin_across(self):
+        self.given().wait_recv()
+        for c in (
+            self.ring(self.s_across, "+z", 3),
+            self.ring(self.s_across, "-z", 4),
+            self.give_on(0),
+            self.give_on(1),
+        ):
+            c.start()
+            self.sent.append(c)
+        self.slots["z"] = 5
+
+    def forward(self, n):
+        fam, found = self.events(n)
+        for s, k, way in found:
+            self.ring(s, way, 0).wait_recv()
+            last = k + 1 == ((4 if fam == 0 else 3) if way == "+z" else (3 if fam == 0 else 4))
+            if not last:
+                c = self.ring(s, way, self.slots["z"])
+                self.slots["z"] += 1
+                c.start()
+                self.sent.append(c)
+            for d in range(4):
+                c = self.first(s, d, self.slots["f"])
+                c.start()
+                self.sent.append(c)
+            self.slots["f"] += 1
+
+    def spread(self, n):
+        fam, found = self.events(n)
+        for s, k, way in found:
+            for d in (2, 3, 0, 1):
+                self.first_in(s, d).wait_recv()
+                c = self.second(s, (d + 2) % 4, self.slots["g"])
+                c.start()
+                self.sent.append(c)
+            self.slots["g"] += 1
+
+    def arrived(self, n):
+        fam, found = self.events(n)
+        for s, k, way in found:
+            for d in range(4):
+                self.second_in(s, d).wait_recv()
+
+    def arrived_across(self):
+        self.local().wait()
+        for d in range(2):
+            self.given_on(d).wait_recv()
+
+    def finish(self):
+        for c in self.sent:
+            c.wait_send()
+
+
+def greet(near, extra=()):
+    barrier = pltpu.get_barrier_semaphore()
+    who = [near[k] for k in ("+x", "-x", "+y", "-y", "+z", "-z", "sibling")] + list(extra)
+    for device in who:
+        pl.semaphore_signal(barrier, inc=1, device_id=device, device_id_type=MESH_ID)
+    pl.semaphore_wait(barrier, len(who))
+
+
+GATHER_SEMS = [
+    pltpu.SemaphoreType.DMA((17,)),
+    pltpu.SemaphoreType.DMA((16,)),
+    pltpu.SemaphoreType.DMA((15, 4)),
+    pltpu.SemaphoreType.DMA((16, 4)),
+    pltpu.SemaphoreType.DMA((14, 4)),
+    pltpu.SemaphoreType.DMA((16, 4)),
+    pltpu.SemaphoreType.DMA,
+]
+
+
+class Project:
+    def __init__(self, at, near, normed, wbuf, part, got, out, sems):
+        self.at, self.near, self.normed, self.wbuf = at, near, normed, wbuf
+        self.part, self.got, self.out, self.ss, self.rs = part, got, out, *sems
+
+    def dot(self, s):
+        w = self.wbuf[s].reshape(2048, 256)
+        return jnp.dot(self.normed[...], w, preferred_element_type=jnp.float32).astype(jnp.bfloat16)
+
+    def copy(self, z):
+        return pltpu.make_async_remote_copy(
+            src_ref=self.part.at[1, z],
+            dst_ref=self.got.at[z],
+            send_sem=self.ss.at[z],
+            recv_sem=self.rs.at[z],
+            device_id=self.near["sibling"],
+            device_id_type=MESH_ID,
+        )
+
+    def columns(self, z):
+        c = self.at["head"]
+        self.part[1, z] = self.dot((1 - c) * NZ + z)
+        self.copy(z).start()
+        self.part[0, z] = self.dot(c * NZ + z)
+
+    def combine(self, z):
+        self.copy(z).wait_recv()
+        total = self.part[0, z].astype(jnp.float32) + self.got[z].astype(jnp.float32)
+        start = pl.multiple_of(z * 256, 256)
+        self.out[:, pl.ds(start, 256)] = total.astype(jnp.bfloat16)
+
+
+def gather_kernel(own, normed, out, wbuf, part, got, *sems):
+    at, near = place()
+    greet(near)
+    gather = Gather(at, near, own, wbuf, sems[:7])
+    proj = Project(at, near, normed, wbuf, part, got, out, sems[7:])
+    z = at["z"]
+    gather.begin()
+    gather.forward(0)
+    gather.begin_across()
+    ready = {1: (1, 2), 3: (2, 3), 5: (3, 4), 7: (4, 5)}
+
+    def columns(lo, hi):
+        for k in range(lo, hi):
+            proj.columns(lax.rem(z + k, NZ))
+            if 0 < k < 4:
+                proj.columns(lax.rem(z + NZ - k, NZ))
+
+    gather.forward(1)
+    gather.spread(0)
+    gather.arrived_across()
+    columns(0, 1)
+    for n in range(2, 8):
+        gather.forward(n)
+        gather.spread(n - 1)
+        gather.arrived(n - 2)
+        if n % 2 == 1:
+            k = (n - 1) // 2
+            columns(k, k + 1)
+    gather.spread(7)
+    gather.arrived(6)
+    gather.arrived(7)
+    columns(4, 5)
+    for k in range(NZ):
+        proj.combine(k)
+    for k in range(NZ):
+        proj.copy(k).wait_send()
+    gather.finish()
+
+
+def project(normed, out_weight):
+    own = out_weight.reshape(16, 128, 256)
+    vmem = pl.BlockSpec(memory_space=pltpu.VMEM)
+    return pl.pallas_call(
+        gather_kernel,
+        out_shape=jax.ShapeDtypeStruct((512, 2048), jnp.bfloat16),
+        in_specs=[pl.BlockSpec(memory_space=pl.ANY), vmem],
+        out_specs=vmem,
+        scratch_shapes=[
+            pltpu.VMEM((16, 16, 128, 256), jnp.bfloat16),
+            pltpu.VMEM((2, NZ, 512, 256), jnp.bfloat16),
+            pltpu.VMEM((NZ, 512, 256), jnp.bfloat16),
+            *GATHER_SEMS,
+            pltpu.SemaphoreType.DMA((NZ,)),
+            pltpu.SemaphoreType.DMA((NZ,)),
+        ],
+        compiler_params=pltpu.CompilerParams(
+            collective_id=0, has_side_effects=True, vmem_limit_bytes=48 << 20
+        ),
+    )(own, normed)
 
 
 def neutral_like(array, identity):
@@ -56,7 +339,9 @@
 
 def block_terms(values_blk, in_blk, out_blk, step_blk, decay_blk, skip_gain):
     heads = decay_blk.shape[1]
-    running = jnp.cumsum(decay_blk, axis=0)
+    steps = jnp.arange(decay_blk.shape[0])
+    lower = (steps[:, None] >= steps[None, :]).astype(jnp.float32)
+    running = jnp.dot(lower, decay_blk, precision=lax.Precision.HIGHEST)
     per_head = values_blk.reshape(values_blk.shape[0], heads, -1)
     scaled = (per_head.astype(jnp.float32) * step_blk[:, :, None]).astype(jnp.bfloat16)
     scores = jnp.dot(out_blk, in_blk.T, preferred_element_type=jnp.float32)
@@ -126,7 +411,7 @@
     out_weight,
     prompt_state,
 ):
-    prompt = lax.all_gather(prompt_state.astype(jnp.bfloat16), "sample", axis=2, tiled=True).astype(
+    prompt = lax.all_gather(prompt_state.astype(jnp.bfloat16), SAMPLE, axis=2, tiled=True).astype(
         prompt_state.dtype
     )
     sweep_sample = partial(local_sweep, skip_gain=skip_gain)
@@ -147,35 +432,30 @@
     outputs = (local_out + carried).reshape(samples * tokens, -1)
     gated = outputs * jax.nn.silu(gate_values.reshape(samples * tokens, -1).astype(jnp.float32))
     normed = group_norm(gated, norm_gain)
-    terms = jnp.dot(
-        normed,
-        lax.all_gather(out_weight, SEQ, axis=1, tiled=True),
-        preferred_element_type=jnp.float32,
-    )
-    mine = sent_and_summed(terms.astype(jnp.bfloat16), "head", 1).astype(jnp.bfloat16)
+    mine = project(normed, out_weight)
     return mine.reshape(samples, tokens, -1)
 
 
 def solution(mesh):
     split = Mesh(
-        mesh.devices.reshape(mesh.shape["sample"], 2, 8, mesh.shape["head"]),
-        ("sample", "seq_0", "seq_1", "head"),
+        mesh.devices.reshape(2, 4, 2, 8, 2),
+        ("ylo", "x", "yhi", "z", "head"),
     )
     return jax.shard_map(
         shards,
         mesh=split,
         in_specs=(
-            P("sample", SEQ, "head"),
-            P("sample", SEQ, "head"),
-            P("sample", SEQ, None),
-            P("sample", SEQ, None),
-            P("sample", SEQ, "head"),
-            P("sample", SEQ, "head"),
+            P(SAMPLE, SEQ, "head"),
+            P(SAMPLE, SEQ, "head"),
+            P(SAMPLE, SEQ, None),
+            P(SAMPLE, SEQ, None),
+            P(SAMPLE, SEQ, "head"),
+            P(SAMPLE, SEQ, "head"),
             P("head"),
             P("head"),
             P("head", SEQ),
-            P("head", None, "sample"),
+            P("head", None, SAMPLE),
         ),
-        out_specs=P("sample", SEQ, "head"),
+        out_specs=P(SAMPLE, SEQ, "head"),
         check_vma=False,
     )

time: 402 us -> 282 us (0.70)
  waiting for transfers between devices: 257 us -> 27.1 us
  Pallas kernels: 0 us -> 102 us
  local copies, waits for them, and re-layouts: 23.9 us -> 55 us
  matrix products: 25.6 us -> 14.8 us
  blocking collectives: 57.1 us -> 47.3 us
    all_gather x1 -> x0, waiting for transfers between devices: 214 us -> none  [shards(): lax.all_gather(out_weight, SEQ, axis=1, tiled=True)]
    pallas_call x0 -> x1, Pallas kernels: none -> 102 us  [project(): pl.pallas_call(gather_kernel, out_shape=jax.ShapeDtypeStruct((512, 2048),...]
    reshape x3 -> x2, local copies, waits for them, and re-layouts: 0.32 us -> 17.1 us  [shards(): outputs = (local_out + carried).reshape(samples * tokens, -1)]
    all_gather x2, waiting for transfers between devices: 42.6 us -> 27 us  [entering(): lax.all_gather(part.astype(kind), axis)]
    dot_general x1 -> x2, matrix products: 13.2 us -> 0.52 us  [block_terms(): running = jnp.dot(lower, decay_blk, precision=lax.Precision.HIGHEST)]
    convert_element_type x1 -> x2, local copies, waits for them, and re-layouts: 4.02 us -> 15.3 us  [shards(): gate_values.reshape(samples * tokens, -1).astype(jnp.float32)]
    all_to_all x1 -> x0, blocking collectives: 10.8 us -> none  [sent_and_summed(): tiles = lax.all_to_all(in_blocks(array, dim, peers), axis, 0, 0, tiled=True)]
    reduce_sum x1 -> x0, other arithmetic: 5.08 us -> none  [sent_and_summed(): return jnp.sum(tiles.astype(jnp.float32), axis=0)]
  transfers between devices with their start and end apart: 3 -> 2, of which waited for: 2 -> 2; matrix products, arithmetic and copies ran while one was open for 7% -> 6% of each run, Pallas kernels for 0% -> 0%
where the time goes in v1:
time: 282 us
  Pallas kernels  102 us (36%)
  local copies, waits for them, and re-layouts  55 us (20%)
  blocking collectives  47.3 us (17%)
  waiting for transfers between devices  27.1 us (10%)
  other arithmetic  21.6 us (8%)
  matrix products  14.8 us (5%)
  between operations  13.6 us (5%)
    pallas_call x1, Pallas kernels, project(): pl.pallas_call(gather_kernel, out_shape=jax.ShapeDtypeStruct((512, 2048),...  102 us
    all_gather x2, waiting for transfers between devices, entering(): lax.all_gather(part.astype(kind), axis)  27 us
    all_gather x1, blocking collectives, shards(): lax.all_gather(prompt_state.astype(jnp.bfloat16), SAMPLE, axis=2, tiled=T...  26.6 us
    all_gather x2, blocking collectives, entering(): lax.all_gather(part.astype(kind), axis)  20.7 us
    reshape x2, local copies, waits for them, and re-layouts, shards(): outputs = (local_out + carried).reshape(samples * tokens, -1)  17.1 us
    convert_element_type x2, local copies, waits for them, and re-layouts, shards(): gate_values.reshape(samples * tokens, -1).astype(jnp.float32)  15.3 us
    unnamed x18, local copies, waits for them, and re-layouts  6.31 us
  transfers between devices with their start and end apart: 2, of which 2 were waited for; matrix products, arithmetic and copies ran while one was open for 6% of the time, Pallas kernels for 0%

profile of v1, /device:TPU:1, one launch (start us, length us, event | category | flops | bytes accessed | tf_op | source)
XLA Modules:
  0.0 281.7 jit_solution(13118075379693351892)
XLA Ops:
  6.5 1.0 copy.25
  7.5 0.9 reshape.530
  8.4 30.5 %while.21 = (s32[]{:T(128)}, f32[1,32,64,128]{3,2,1,0:T(8,128)S(1)}, f32[1,32]{0,1:T(8,128)S(1)}, f32[2,1,256,32,64]{2,4,3,1,0:T(8,128)}, f32[2,1,256,32]{2,3,1,...) while((s32[]{:T(128)}, ...), condition=%wide.region_1.2_spmd.clone, body=%wide.region_0.1_spmd.clone.sunk | while | flops 459939904 | bytes 82679640 | solution.py:385
  8.5 1.1 bitcast_dynamic-update-slice_fusion.5
  9.5 0.3 bitcast_dynamic-update-slice_fusion.4
  9.8 0.2 exponential_reduce_fusion.2
  10.1 0.2 mul.837
  10.4 1.5 mul.838
  11.9 1.1 constant_dynamic-slice_fusion.5
  12.9 1.5 copy.52
  14.4 2.0 multiply_convert_fusion.13
  16.4 1.4 fusion.104
  17.9 0.2 convert_element_type.804
  18.0 0.2 fusion.105
  18.3 0.8 copy-done.15
  19.1 2.3 fusion.106
  21.4 1.9 copy-done.16
  23.4 1.1 bitcast_dynamic-update-slice_fusion.5
  24.5 0.3 bitcast_dynamic-update-slice_fusion.4
  24.7 0.2 exponential_reduce_fusion.2
  25.1 0.2 mul.837
  25.3 1.5 mul.838
  26.8 1.1 constant_dynamic-slice_fusion.5
  27.9 1.5 copy.52
  29.4 2.0 multiply_convert_fusion.13
  31.4 2.8 fusion.104
  34.3 0.2 fusion.105
  34.6 2.3 fusion.106
  37.0 1.9 copy-done.16
  38.9 0.9 convert_element_type.465
  40.0 16.1 %all-gather.2 = bf16[8,1,32]{2,1,0:T(2,128)(2,1)S(1)} all-gather(bf16[1,1,32]{2,1,0:T(2,128)(2,1)S(1)} %bitcast.412), channel_id=2, replica_groups=mesh['ylo'=2,'x'=4,'yhi'=2,'z'=8,'head'=2] {'z'}, dimensions={0}, use_global_device_ids=true | all-gather | bytes 576 | tf_op jit(solution)/shard_map/all_gather | solution.py:313
  56.1 4.6 %all_gather.25 = bf16[2,1,32]{2,1,0:T(2,128)(2,1)S(1)} all-gather(bf16[1,1,32]{2,1,0:T(2,128)(2,1)S(1)} %fusion.82), channel_id=1, replica_groups=mesh['ylo'=2,'x'=4,'yhi'=2,'z'=8,'head'=2] {'yhi'}, dimensions={0}, use_global_device_ids=true | all-gather | bytes 192 | tf_op jit(solution)/shard_map/all_gather | solution.py:313
  60.7 7.4 %reshape.653 = f32[2,256,32,64]{3,2,1,0:T(8,128)} reshape(bf16[1,512,2048]{2,1,0:T(8,128)(2,1)} %param.13) | data formatting | bytes 6291456 | tf_op jit(solution)/shard_map/convert_element_type | solution.py:433
  68.1 7.9 %copy.34 = f32[2,256,32,64]{1,3,2,0:T(8,128)} copy(f32[2,256,32,64]{3,2,1,0:T(8,128)} %reshape.653) | data formatting | bytes 8388608 | tf_op jit(solution)/shard_map/convert_element_type | solution.py:433
  76.1 22.5 %all-gather.8.cloned.1.call-done = bf16[8,32,64,128]{3,2,1,0:T(8,128)(2,1)} async-done(((bf16[1,32,64,128]{3,2,1,0:T(8,128)(2,1)}), bf16[8,32,64,128]{3,2,1,0:T(8,128)(2,1)}) %all-gather.8.cloned.1.call-update) | async-done | bytes 4194320 | tf_op jit(solution)/shard_map/all_gather | solution.py:313
  98.6 3.4 %fusion.75 = bf16[1,1,32,64,128]{4,3,2,1,0:T(8,128)(2,1)} fusion(f32[32]{0:T(128)S(1)} %bitcast_multiply_fusion.5, f32[32]{0:T(128)S(1)} %get-tuple-element.186, f32[32]{0:T(128)S(1)} %get-tuple-element.191, f32[32]{0:T(128)S(1)} %get-tuple-element.190, f32[32]{0:T(128)S(1)} %get-tuple-element.189, f32[32]{0:T(128)S(1)} %get-tuple-element.188, ...), kind=kLoop, calls=%fused_computation.115 | loop fusion | flops 6291456 | bytes 4719616 | tf_op jit(solution)/shard_map/convert_element_type | solution.py:313
  102.0 26.6 %all_gather.29 = bf16[32,64,128]{1,0,2:T(8,128)(2,1)S(1)} all-gather(bf16[32,64,16]{1,0,2:T(8,128)(2,1)S(1)} %copy.47), channel_id=1, replica_groups=mesh['ylo'=2,'x'=4,'yhi'=2,'z'=8,'head'=2] {'ylo','x'}, dimensions={2}, use_global_device_ids=true | all-gather | bytes 589824 | tf_op jit(solution)/shard_map/all_gather | solution.py:414
  128.6 1.1 copy.29
  129.8 4.5 %all-gather.6.cloned.1.call-done = bf16[2,1,32,64,128]{4,3,2,1,0:T(8,128)(2,1)} async-done(((bf16[1,1,32,64,128]{4,3,2,1,0:T(8,128)(2,1)}), bf16[2,1,32,64,128]{4,3,2,1,0:T(8,128)(2,1)}) %all-gather.6.cloned.1.call-update) | async-done | bytes 1048592 | tf_op jit(solution)/shard_map/all_gather | solution.py:313
  134.3 4.9 %fusion.60 = f32[32,64,128]{2,1,0:T(8,128)S(1)} fusion(bf16[32,64,128]{2,1,0:T(8,128)(2,1)S(1)} %copy.29, bf16[2,1,32,64,128]{4,3,2,1,0:T(8,128)(2,1)} %all-gather.6.cloned.1.call-done, f32[32]{0:T(128)S(1)} %get-tuple-element.179, f32[32]{0:T(128)S(1)} %bitcast_multiply_fusion.5, f32[32]{0:T(128)S(1)} %get-tuple-element.186, f32[32]{0:T(128)S(1)} %get-tuple-element.191, ...), kind=kLoop, calls=%fused_computation.99 | loop fusion | flops 11272192 | bytes 6817290 | tf_op jit(solution)/shard_map/add | solution.py:423
  139.3 5.0 %multiply_reduce_fusion = (f32[2,256,32]{1,2,0:T(8,128)S(1)}, f32[2,256,32,64]{1,3,2,0:T(8,128)}) fusion(f32[2,256,32,64]{1,3,2,0:T(8,128)S(1)} %copy-done.5, bf16[2,256,128,1]{2,1,3,0:T(8,128)(2,1)S(1)} %bitcast.411, f32[2,1,32,64,128]{4,3,2,1,0:T(8,128)S(1)} %copy-done.13, f32[32,64,128]{2,1,0:T(8,128)S(1)} %fusion.60, f32[2,32]{1,0:T(2,128)S(1)} %bitcast.413, ...), kind=kOutput, calls=%fused_computation.52 | convolution fusion | flops 279429120 | bytes 15991040 | tf_op jit(solution)/shard_map/sktn,skhpn->skthp/dot_general | solution.py:429
  144.6 0.7 mul.499
  145.3 3.9 %copy.44 = f32[64,8,4,512]{3,1,2,0:T(8,128)} copy(f32[64,8,4,512]{3,2,1,0:T(4,128)S(1)} %bitcast.402) | data formatting | bytes 8388608
  149.2 9.1 %copy.38 = f32[2,256,32,64]{3,2,1,0:T(8,128)} copy(f32[2,256,32,64]{1,3,2,0:T(8,128)} %get-tuple-element.193) | data formatting | bytes 8388608 | tf_op jit(solution)/shard_map/reshape | solution.py:432
  158.3 8.0 %reshape.652 = f32[512,2048]{1,0:T(8,128)} reshape(f32[2,256,32,64]{3,2,1,0:T(8,128)} %copy.38) | data formatting | bytes 8388608 | tf_op jit(solution)/shard_map/reshape | solution.py:432
  166.3 5.1 %fusion.31.normed = bf16[512,2048]{1,0:T(8,128)(2,1)S(1)} fusion(f32[512,2048]{1,0:T(8,128)} %bitcast.403, f32[512,2048]{1,0:T(8,128)} %reshape.652, f32[2048]{0:T(1024)S(1)} %copy-done.12, bf16[1,512,2048]{2,1,0:T(8,128)(2,1)S(1)} %copy-done.4), kind=kLoop, calls=%fused_computation.53 | loop fusion | flops 9437184 | bytes 12591104 | tf_op jit(solution)/shard_map/convert_element_type | solution.py:399
  171.5 102.1 %shard_map.100 = bf16[512,2048]{1,0:T(8,128)(2,1)S(1)} custom-call(bf16[16,128,256]{2,1,0:T(8,128)(2,1)S(1)} %bitcast.396, bf16[512,2048]{1,0:T(8,128)(2,1)S(1)} %fusion.31.normed), custom_call_target="tpu_custom_call" | custom-call | tf_op jit(solution)/shard_map/pallas_call | solution.py:282
  273.6 1.3 copy.79
  (87 shorter events, 1.2 us)
Async XLA Ops:
  6.5 92.1 %all-gather.8.cloned.1.call-start = ((), (), s32[]{:S(2)}) async-start(), calls=%async_computation.1 | async-start | bytes 4718592 | tf_op jit(solution)/shard_map/all_gather | solution.py:313
  8.4 1.6 copy-start.1
  8.4 1.6 copy-start.7
  8.4 3.4 %copy-start.3 = (bf16[2,1,256,2048]{3,2,0,1:T(8,128)(2,1)S(1)}, bf16[2,1,256,2048]{3,2,0,1:T(8,128)(2,1)}, u32[]{:S(2)}) copy-start(bf16[2,1,256,2048]{3,2,0,1:T(8,128)(2,1)} %get-tuple-element.323) | copy-start | bytes 6291460 | tf_op jit(solution)/shard_map/vmap()/while
  12.9 3.5 %copy-start.6 = (bf16[2,1,256,128]{3,2,1,0:T(8,128)(2,1)S(1)}, bf16[2,1,256,128]{3,2,1,0:T(8,128)(2,1)}, u32[]{:S(2)}) copy-start(bf16[2,1,256,128]{3,2,1,0:T(8,128)(2,1)} %get-tuple-element.325) | copy-start | bytes 393220 | tf_op jit(solution)/shard_map/vmap()/while
  16.4 1.6 copy-start.9
  16.4 1.9 copy-start.14
  16.4 2.6 copy-start.15
  19.1 4.3 %copy-start.2 = (f32[1,32,64,128]{3,2,1,0:T(8,128)S(1)}, f32[1,32,64,128]{3,2,1,0:T(8,128)}, u32[]{:S(2)}) copy-start(f32[1,32,64,128]{3,2,1,0:T(8,128)} %fusion.104) | copy-start | bytes 3145732 | tf_op jit(solution)/shard_map/vmap()/while
  19.1 4.3 %copy-start.8 = (f32[2,1,256,32]{3,2,1,0:T(8,128)S(1)}, f32[2,1,256,32]{3,2,1,0:T(8,128)}, u32[]{:S(2)}) copy-start(f32[2,1,256,32]{3,2,1,0:T(8,128)} %copy-done.7) | copy-start | bytes 196612 | tf_op jit(solution)/shard_map/vmap()/while
  21.4 2.0 copy-start.16
  23.4 1.6 copy-start.1
  23.4 1.6 copy-start.7
  23.4 3.4 %copy-start.3 = (bf16[2,1,256,2048]{3,2,0,1:T(8,128)(2,1)S(1)}, bf16[2,1,256,2048]{3,2,0,1:T(8,128)(2,1)}, u32[]{:S(2)}) copy-start(bf16[2,1,256,2048]{3,2,0,1:T(8,128)(2,1)} %get-tuple-element.323) | copy-start | bytes 6291460 | tf_op jit(solution)/shard_map/vmap()/while
  27.9 3.5 %copy-start.6 = (bf16[2,1,256,128]{3,2,1,0:T(8,128)(2,1)S(1)}, bf16[2,1,256,128]{3,2,1,0:T(8,128)(2,1)}, u32[]{:S(2)}) copy-start(bf16[2,1,256,128]{3,2,1,0:T(8,128)(2,1)} %get-tuple-element.325) | copy-start | bytes 393220 | tf_op jit(solution)/shard_map/vmap()/while
  31.3 3.0 %copy-start.9 = (bf16[2,1,256,128]{3,2,1,0:T(8,128)(2,1)S(1)}, bf16[2,1,256,128]{3,2,1,0:T(8,128)(2,1)}, u32[]{:S(2)}) copy-start(bf16[2,1,256,128]{3,2,1,0:T(8,128)(2,1)} %get-tuple-element.326) | copy-start | bytes 393220 | tf_op jit(solution)/shard_map/vmap()/while
  31.3 3.2 %copy-start.14 = (f32[32]{0:T(128)S(1)}, f32[32]{0:T(128)}, u32[]{:S(2)}) copy-start(f32[32]{0:T(128)} %get-tuple-element.327) | copy-start | bytes 388 | tf_op jit(solution)/shard_map/vmap()/while
  31.4 3.2 %copy-start.15 = (f32[2,1,256,32,64]{2,4,3,1,0:T(8,128)S(1)}, f32[2,1,256,32,64]{2,4,3,1,0:T(8,128)}, u32[]{:S(2)}) copy-start(f32[2,1,256,32,64]{2,4,3,1,0:T(8,128)} %get-tuple-element.303) | copy-start | bytes 12582916 | tf_op jit(solution)/shard_map/vmap()/while
  34.6 4.3 %copy-start.2 = (f32[1,32,64,128]{3,2,1,0:T(8,128)S(1)}, f32[1,32,64,128]{3,2,1,0:T(8,128)}, u32[]{:S(2)}) copy-start(f32[1,32,64,128]{3,2,1,0:T(8,128)} %fusion.104) | copy-start | bytes 3145732 | tf_op jit(solution)/shard_map/vmap()/while
  34.6 4.3 %copy-start.8 = (f32[2,1,256,32]{3,2,1,0:T(8,128)S(1)}, f32[2,1,256,32]{3,2,1,0:T(8,128)}, u32[]{:S(2)}) copy-start(f32[2,1,256,32]{3,2,1,0:T(8,128)} %copy-done.7) | copy-start | bytes 196612 | tf_op jit(solution)/shard_map/vmap()/while
  36.9 2.0 copy-start.16
  39.8 94.5 %all-gather.6.cloned.1.call-start = ((), (), s32[]{:S(2)}) async-start(), calls=%async_computation | async-start | bytes 1572864 | tf_op jit(solution)/shard_map/all_gather | solution.py:313
  68.1 7.9 %copy-start.11 = (f32[32,64,16]{1,2,0:T(8,128)S(1)}, f32[32,64,16]{1,2,0:T(8,128)}, u32[]{:S(2)}) copy-start(f32[32,64,16]{1,2,0:T(8,128)} %param.21) | copy-start | bytes 393220
  128.6 10.6 %copy-start.10 = (bf16[2,1,256,128]{3,2,1,0:T(8,128)(2,1)S(1)}, bf16[2,1,256,128]{3,2,1,0:T(8,128)(2,1)}, u32[]{:S(2)}) copy-start(bf16[2,1,256,128]{3,2,1,0:T(8,128)(2,1)} %get-tuple-element.338) | copy-start | bytes 393220
  134.3 4.9 %copy-start.5 = (f32[2,256,32,64]{1,3,2,0:T(8,128)S(1)}, f32[2,256,32,64]{1,3,2,0:T(8,128)}, u32[]{:S(2)}) copy-start(f32[2,256,32,64]{1,3,2,0:T(8,128)} %copy.34) | copy-start | bytes 12582916
  134.3 4.9 %copy-start.13 = (f32[2,1,32,64,128]{4,3,2,1,0:T(8,128)S(1)}, f32[2,1,32,64,128]{4,3,2,1,0:T(8,128)}, u32[]{:S(2)}) copy-start(f32[2,1,32,64,128]{4,3,2,1,0:T(8,128)} %get-tuple-element.79) | copy-start | bytes 6291460
  158.3 8.0 %copy-start.4 = (bf16[1,512,2048]{2,1,0:T(8,128)(2,1)S(1)}, bf16[1,512,2048]{2,1,0:T(8,128)(2,1)}, u32[]{:S(2)}) copy-start(bf16[1,512,2048]{2,1,0:T(8,128)(2,1)} %param.13) | copy-start | bytes 6291460
  158.3 8.0 %copy-start.12 = (f32[2048]{0:T(1024)S(1)}, f32[2048]{0:T(1024)}, u32[]{:S(2)}) copy-start(f32[2048]{0:T(1024)} %param.19) | copy-start | bytes 24580
  166.3 5.1 %copy-start = (bf16[2048,256]{1,0:T(8,128)(2,1)S(1)}, bf16[2048,256]{1,0:T(8,128)(2,1)}, u32[]{:S(2)}) copy-start(bf16[2048,256]{1,0:T(8,128)(2,1)} %param.20) | copy-start | bytes 3145732
Sparse Core Ops, SparseCore 0:
  39.9 58.6 all-gather.7
  102.2 32.1 all-gather.5

commit v2 on v1

--- a/solution.py
+++ b/solution.py
@@ -186,12 +186,23 @@
             c.wait_send()
 
 
-def greet(near, extra=()):
+def greet(at, near):
     barrier = pltpu.get_barrier_semaphore()
-    who = [near[k] for k in ("+x", "-x", "+y", "-y", "+z", "-z", "sibling")] + list(extra)
+    who = [near["across"], near["sibling"], {"yhi": 1 - at["yhi"]}]
+    who += [near_z(at, k) for k in range(1, NZ)]
+    who += [near_sample(at, k) for k in range(1, 8)]
     for device in who:
         pl.semaphore_signal(barrier, inc=1, device_id=device, device_id_type=MESH_ID)
     pl.semaphore_wait(barrier, len(who))
+
+
+def near_z(at, k):
+    return {"z": lax.rem(at["z"] + k, NZ)}
+
+
+def near_sample(at, k):
+    ylo = at["ylo"] if k < 4 else 1 - at["ylo"]
+    return {"ylo": ylo, "x": lax.rem(at["x"] + k % 4, 4)}
 
 
 GATHER_SEMS = [
@@ -237,166 +248,348 @@
         self.out[:, pl.ds(start, 256)] = total.astype(jnp.bfloat16)
 
 
-def gather_kernel(own, normed, out, wbuf, part, got, *sems):
+F32, BF16 = jnp.float32, jnp.bfloat16
+NT = (((1,), (1,)), ((), ()))
+
+
+def mm(a, b):
+    return jnp.dot(a, b, preferred_element_type=F32)
+
+
+def three(v):
+    a = v.astype(BF16)
+    rest = v - a.astype(F32)
+    b = rest.astype(BF16)
+    return a, b, (rest - b.astype(F32)).astype(BF16)
+
+
+def by_column(v, e):
+    a, b, c = three(v)
+    return mm(a, e) + mm(b, e) + mm(c, e)
+
+
+def iota(shape, dim):
+    return lax.broadcasted_iota(jnp.int32, shape, dim)
+
+
+def remote(src, dst, send, recv, to):
+    return pltpu.make_async_remote_copy(
+        src_ref=src,
+        dst_ref=dst,
+        send_sem=send,
+        recv_sem=recv,
+        device_id=to,
+        device_id_type=MESH_ID,
+    )
+
+
+class Scan:
+    def __init__(self, at, sout, sin, dsend, din, init, tsend, eout, entry, sems):
+        self.at = at
+        self.sout, self.sin, self.dsend, self.din = sout, sin, dsend, din
+        self.init, self.tsend, self.eout, self.entry = init, tsend, eout, entry
+        self.ss, self.sr, self.ds, self.dr, self.es, self.er, self.ps, self.ir, self.ts = sems
+
+    def peer(self, k):
+        return lax.rem(self.at["z"] + k, NZ)
+
+    def state(self, k):
+        z, to = self.at["z"], self.peer(k)
+        return remote(self.sout.at[to], self.sin.at[z], self.ss.at[k], self.sr.at[z], {"z": to})
+
+    def state_in(self, k):
+        z = self.peer(k)
+        return remote(self.sout.at[z], self.sin.at[z], self.ss.at[k], self.sr.at[z], {"z": z})
+
+    def decay(self, k):
+        z, to = self.at["z"], self.peer(k)
+        return remote(self.dsend.at[0], self.din.at[z], self.ds.at[k], self.dr.at[z], {"z": to})
+
+    def decay_in(self, k):
+        z = self.peer(k)
+        return remote(self.dsend.at[0], self.din.at[z], self.ds.at[k], self.dr.at[z], {"z": z})
+
+    def entering(self, k):
+        z, to = self.at["z"], self.peer(k)
+        return remote(self.eout.at[to], self.entry.at[z], self.es.at[k], self.er.at[z], {"z": to})
+
+    def entering_in(self, k):
+        z = self.peer(k)
+        return remote(self.eout.at[z], self.entry.at[z], self.es.at[k], self.er.at[z], {"z": z})
+
+    def prompt(self, k):
+        return remote(
+            self.tsend, self.init, self.ps.at[k], self.ir, near_sample(self.at, k)
+        )
+
+    def total(self):
+        return remote(self.tsend, self.init, self.ts, self.ir, {"yhi": 1 - self.at["yhi"]})
+
+    def holds_prompt(self):
+        m = self.at["ylo"] * 4 + self.at["x"]
+        return (m == self.at["z"]) & (self.at["yhi"] == 0)
+
+    def send_prompt(self, prompt_hbm, prompt_vmem, sem):
+        @pl.when(self.holds_prompt())
+        def _():
+            load = pltpu.make_async_copy(prompt_hbm, prompt_vmem, sem)
+            load.start()
+            load.wait()
+            eye = (iota((16, 16), 0) == iota((16, 16), 1)).astype(F32).astype(BF16)
+            low = prompt_vmem[...].astype(BF16)
+            turned = lax.dot_general(eye, low, NT, preferred_element_type=F32).astype(BF16)
+            self.tsend[...] = turned
+            self.init[...] = turned
+            for k in range(1, 8):
+                self.prompt(k).start()
+
+    def send_states(self):
+        for k in range(1, NZ):
+            self.state(k).start()
+            self.decay(k).start()
+        z = self.at["z"]
+        self.sin[z] = self.sout[z]
+        self.din[z] = self.dsend[0]
+
+    def combine(self, hi):
+        @pl.when(self.at["yhi"] == hi)
+        def _():
+            for k in range(1, NZ):
+                self.state_in(k).wait_recv()
+                self.decay_in(k).wait_recv()
+            if hi == 0:
+                @pl.when(self.holds_prompt())
+                def _():
+                    for k in range(1, 8):
+                        self.prompt(k).wait_send()
+
+                @pl.when(jnp.logical_not(self.holds_prompt()))
+                def _():
+                    self.prompt(1).wait_recv()
+            else:
+                self.total().wait_recv()
+
+            def step(j, acc):
+                self.eout[j] = acc.astype(BF16)
+                return acc * self.din[j] + self.sin[j].astype(F32)
+
+            acc = lax.fori_loop(0, NZ, step, self.init[...].astype(F32))
+            if hi == 0:
+                self.tsend[...] = acc.astype(BF16)
+                self.total().start()
+            for k in range(1, NZ):
+                self.entering(k).start()
+            z = self.at["z"]
+            self.entry[z] = self.eout[z]
+
+    def entered(self):
+        for k in range(1, NZ):
+            self.entering_in(k).wait_recv()
+
+    def finish(self):
+        for k in range(1, NZ):
+            self.state(k).wait_send()
+            self.decay(k).wait_send()
+            self.entering(k).wait_send()
+
+        @pl.when(self.at["yhi"] == 0)
+        def _():
+            self.total().wait_send()
+
+
+SCAN_SEMS = [pltpu.SemaphoreType.DMA((NZ,))] * 7 + [pltpu.SemaphoreType.DMA] * 2
+
+
+class Local:
+    def __init__(self, **refs):
+        self.__dict__.update(refs)
+
+    def prepare(self):
+        self.e[...] = (iota((32, 2048), 0) == lax.shift_right_logical(iota((32, 2048), 1), 6)).astype(F32).astype(BF16)
+        tri = (iota((L, L), 0) >= iota((L, L), 1)).astype(F32).astype(BF16)
+        eye = (iota((32, 32), 0) == iota((32, 32), 1)).astype(F32).astype(BF16)
+        self.bt[...] = self.b_in[...].astype(F32).T.astype(BF16)
+        for b in range(2):
+            rows = slice(b * L, b * L + L)
+            parts = three(self.log_decay[rows])
+            run = sum(mm(tri, part) for part in parts)
+            self.run[rows] = run
+            turned = [lax.dot_general(eye, part, NT, preferred_element_type=F32) for part in three(run)]
+            self.runt[b] = turned[0] + turned[1] + turned[2]
+            self.scores[b] = mm(self.c_out[rows], self.bt[:, rows])
+        ends = [self.run[L - 1 : L], self.run[2 * L - 1 : 2 * L]]
+        line = iota((8, 32), 0)
+        self.lines[...] = jnp.where(
+            line == 0,
+            jnp.exp(ends[0]),
+            jnp.where(
+                line == 1,
+                jnp.exp(ends[1]),
+                jnp.where(line == 2, jnp.exp(ends[0] + ends[1]), self.skip_gain[...]),
+            ),
+        )
+
+    def states(self, lo, hi):
+        def group(g, _):
+            cols = pl.ds(pl.multiple_of(g * 512, 512), 512)
+            e = self.e[:, cols]
+            wide = by_column(self.lines[...], e)
+            self.wide[:, cols] = wide
+            self.dsend[0, :, cols] = wide[2:3]
+            found = []
+            for b in range(2):
+                rows = slice(b * L, b * L + L)
+                run = self.run[rows]
+                self.re[rows, cols] = by_column(run, e)
+                scaled = (self.values[rows, cols].astype(F32) * by_column(self.step[rows], e)).astype(BF16)
+                self.scaled[rows, cols] = scaled
+                tail = by_column(jnp.exp(run[L - 1 : L] - run), e)
+                weighted = (scaled.astype(F32) * tail).astype(BF16)
+                found.append(mm(self.bt[:, rows], weighted))
+            self.bs0[:, cols] = found[0]
+            state = (wide[1:2] * found[0] + found[1]).astype(BF16)
+            self.sout[:, :, cols] = state.reshape(NZ, 16, 512)
+            return 0
+
+        lax.fori_loop(lo, hi, group, 0)
+
+    def mix(self, b, lo, hi):
+        half = L // 2
+        keep = iota((half, half), 0) >= iota((half, half), 1)
+        first = iota((L, 128), 1) < P_SIZE
+        rows = slice(b * L, b * L + L)
+
+        def pair(j, _):
+            cols = pl.ds(pl.multiple_of(j * 128, 128), 128)
+            scaled = self.scaled[rows, cols]
+            re = self.re[rows, cols]
+            made = []
+            for one in range(2):
+                col = re[:, one * P_SIZE : one * P_SIZE + 1]
+                row = self.runt[b, pl.ds(2 * j + one, 1), :]
+                top = jnp.exp(jnp.where(keep, col[:half] - row[:, :half], -1e30))
+                top = (self.scores[b, :half, :half] * top).astype(BF16)
+                left = jnp.exp(col[half:] - row[:, :half])
+                left = (self.scores[b, half:, :half] * left).astype(BF16)
+                right = jnp.exp(jnp.where(keep, col[half:] - row[:, half:], -1e30))
+                right = (self.scores[b, half:, half:] * right).astype(BF16)
+                under = mm(jnp.concatenate([left, right], axis=1), scaled)
+                made.append(jnp.concatenate([mm(top, scaled[:half]), under], axis=0))
+            self.lout[rows, cols] = jnp.where(first, made[0], made[1])
+            return 0
+
+        lax.fori_loop(lo, hi, pair, 0)
+
+    def normalize(self, b, lo, hi):
+        def group(g, _):
+            cols = pl.ds(pl.multiple_of(g * 512, 512), 512)
+            start = self.entry[:, :, cols].reshape(128, 512)
+            if b == 1:
+                start = (self.wide[0:1, cols] * start.astype(F32) + self.bs0[:, cols]).astype(BF16)
+            for r in range(b * L, b * L + L, 128):
+                rows = slice(r, r + 128)
+                carried = jnp.exp(self.re[rows, cols]) * mm(self.c_out[rows], start)
+                out = self.lout[rows, cols] + self.wide[3:4, cols] * self.values[rows, cols].astype(F32)
+                out = out + carried
+                v = self.gate[rows, cols].astype(F32)
+                gated = out * (0.5 * v * (1.0 + jnp.tanh(0.5 * v)))
+                mean = jnp.sum(gated * gated, axis=1, keepdims=True) * (1.0 / 512)
+                scaled = gated * lax.rsqrt(mean + EPSILON) * self.norm_gain[:, cols]
+                self.normed[rows, cols] = scaled.astype(BF16)
+            return 0
+
+        lax.fori_loop(lo, hi, group, 0)
+
+
+def kernel(
+    own, values_hbm, gate_hbm, prompt_hbm, b_in, c_out, step, log_decay, skip_gain, norm_gain,
+    result,
+    wbuf, part, got, values, gate, scaled, re, lout, normed, bs0, scores, run, runt, e, bt,
+    lines, wide, sout, sin, dsend, din, init, tsend, eout, entry, prompt, load, *sems,
+):
     at, near = place()
-    greet(near)
+    first = pltpu.make_async_copy(values_hbm, values, load.at[0])
+    second = pltpu.make_async_copy(gate_hbm, gate, load.at[1])
+    first.start()
+    second.start()
+    greet(at, near)
     gather = Gather(at, near, own, wbuf, sems[:7])
-    proj = Project(at, near, normed, wbuf, part, got, out, sems[7:])
+    scan = Scan(at, sout, sin, dsend, din, init, tsend, eout, entry, sems[7:16])
+    proj = Project(at, near, normed, wbuf, part, got, result, sems[16:18])
+    local = Local(
+        b_in=b_in, c_out=c_out, step=step, log_decay=log_decay, skip_gain=skip_gain, norm_gain=norm_gain,
+        values=values, gate=gate, scaled=scaled, re=re, lout=lout, normed=normed, bs0=bs0, scores=scores,
+        run=run, runt=runt, e=e, bt=bt, lines=lines, wide=wide, sout=sout, dsend=dsend, entry=entry,
+    )
     z = at["z"]
+
+    def columns(k):
+        proj.columns(lax.rem(z + k, NZ))
+        if 0 < k < 4:
+            proj.columns(lax.rem(z + NZ - k, NZ))
+
+    def combine(k):
+        proj.combine(lax.rem(z + k, NZ))
+        if 0 < k < 4:
+            proj.combine(lax.rem(z + NZ - k, NZ))
+
     gather.begin()
+    scan.send_prompt(prompt_hbm, prompt, load.at[2])
+    local.prepare()
+    first.wait()
+    local.states(0, 2)
     gather.forward(0)
+    local.states(2, 4)
+    scan.send_states()
     gather.begin_across()
-    ready = {1: (1, 2), 3: (2, 3), 5: (3, 4), 7: (4, 5)}
-
-    def columns(lo, hi):
-        for k in range(lo, hi):
-            proj.columns(lax.rem(z + k, NZ))
-            if 0 < k < 4:
-                proj.columns(lax.rem(z + NZ - k, NZ))
-
+    local.mix(0, 0, 8)
     gather.forward(1)
     gather.spread(0)
+    local.mix(0, 8, 16)
+    scan.combine(0)
+    gather.forward(2)
+    gather.spread(1)
+    local.mix(1, 0, 8)
+    scan.combine(1)
+    gather.forward(3)
+    gather.spread(2)
+    local.mix(1, 8, 16)
+    second.wait()
+    scan.entered()
+    local.normalize(0, 0, 4)
+    gather.forward(4)
+    gather.spread(3)
+    local.normalize(1, 0, 4)
     gather.arrived_across()
-    columns(0, 1)
-    for n in range(2, 8):
-        gather.forward(n)
-        gather.spread(n - 1)
-        gather.arrived(n - 2)
-        if n % 2 == 1:
-            k = (n - 1) // 2
-            columns(k, k + 1)
+    columns(0)
+    gather.arrived(0)
+    gather.arrived(1)
+    columns(1)
+    gather.forward(5)
+    gather.spread(4)
+    combine(0)
+    combine(1)
+    gather.arrived(2)
+    gather.arrived(3)
+    columns(2)
+    gather.forward(6)
+    gather.spread(5)
+    combine(2)
+    gather.forward(7)
+    gather.spread(6)
+    gather.arrived(4)
+    gather.arrived(5)
+    columns(3)
     gather.spread(7)
+    combine(3)
     gather.arrived(6)
     gather.arrived(7)
-    columns(4, 5)
-    for k in range(NZ):
-        proj.combine(k)
+    columns(4)
+    combine(4)
     for k in range(NZ):
         proj.copy(k).wait_send()
+    scan.finish()
     gather.finish()
-
-
-def project(normed, out_weight):
-    own = out_weight.reshape(16, 128, 256)
-    vmem = pl.BlockSpec(memory_space=pltpu.VMEM)
-    return pl.pallas_call(
-        gather_kernel,
-        out_shape=jax.ShapeDtypeStruct((512, 2048), jnp.bfloat16),
-        in_specs=[pl.BlockSpec(memory_space=pl.ANY), vmem],
-        out_specs=vmem,
-        scratch_shapes=[
-            pltpu.VMEM((16, 16, 128, 256), jnp.bfloat16),
-            pltpu.VMEM((2, NZ, 512, 256), jnp.bfloat16),
-            pltpu.VMEM((NZ, 512, 256), jnp.bfloat16),
-            *GATHER_SEMS,
-            pltpu.SemaphoreType.DMA((NZ,)),
-            pltpu.SemaphoreType.DMA((NZ,)),
-        ],
-        compiler_params=pltpu.CompilerParams(
-            collective_id=0, has_side_effects=True, vmem_limit_bytes=48 << 20
-        ),
-    )(own, normed)
-
-
-def neutral_like(array, identity):
-    return jax.tree.map(
-        lambda a, e: jnp.broadcast_to(jnp.asarray(e, a.dtype), a.shape), array, identity
-    )
-
-
-def entering(array, axes, combine, identity):
-    before = start = neutral_like(array, identity)
-    so_far = array
-    for axis in reversed(axes):
-        peers, index = (lax.axis_size(axis), lax.axis_index(axis))
-        pieces = jax.tree.map(
-            lambda part, kind: lax.all_gather(part.astype(kind), axis),
-            so_far,
-            (jnp.bfloat16, jnp.bfloat16),
-        )
-        inside, so_far = (start, start)
-        for k in range(peers):
-            passed = k < index
-            so_far = combine(
-                so_far, jax.tree.map(lambda part, own: part[k].astype(own.dtype), pieces, array)
-            )
-            inside = jax.tree.map(lambda new, old: jnp.where(passed, new, old), so_far, inside)
-        before = combine(inside, before)
-    return before
-
-
-def in_blocks(array, dim, peers):
-    dims = array.shape
-    tiles = array.reshape(*dims[:dim], peers, dims[dim] // peers, *dims[dim + 1 :])
-    return jnp.moveaxis(tiles, dim, 0)
-
-
-def sent_and_summed(array, axis, dim):
-    peers = lax.axis_size(axis)
-    tiles = lax.all_to_all(in_blocks(array, dim, peers), axis, 0, 0, tiled=True)
-    return jnp.sum(tiles.astype(jnp.float32), axis=0)
-
-
-def block_terms(values_blk, in_blk, out_blk, step_blk, decay_blk, skip_gain):
-    heads = decay_blk.shape[1]
-    steps = jnp.arange(decay_blk.shape[0])
-    lower = (steps[:, None] >= steps[None, :]).astype(jnp.float32)
-    running = jnp.dot(lower, decay_blk, precision=lax.Precision.HIGHEST)
-    per_head = values_blk.reshape(values_blk.shape[0], heads, -1)
-    scaled = (per_head.astype(jnp.float32) * step_blk[:, :, None]).astype(jnp.bfloat16)
-    scores = jnp.dot(out_blk, in_blk.T, preferred_element_type=jnp.float32)
-    token_offset = jnp.arange(values_blk.shape[0])
-    causal = token_offset[:, None] >= token_offset[None, :]
-    by_head = running.T
-    spread = by_head[:, :, None] - by_head[:, None, :]
-    pair_decay = jnp.exp(jnp.where(causal[None], spread, -1e30))
-    mixing = (scores[None] * pair_decay).astype(jnp.bfloat16)
-    inner = jnp.einsum("hts,shp->thp", mixing, scaled, preferred_element_type=jnp.float32)
-    tail = jnp.exp(running[-1][None, :] - running)
-    weighted = (scaled.astype(jnp.float32) * tail[:, :, None]).astype(jnp.bfloat16)
-    block_state = jnp.einsum("shp,sn->hpn", weighted, in_blk, preferred_element_type=jnp.float32)
-    local_out = inner + skip_gain[None, :, None] * per_head.astype(jnp.float32)
-    return (local_out, running, block_state)
-
-
-def local_sweep(values_s, in_s, out_s, step_s, decay_s, skip_gain):
-    count = values_s.shape[0] // L
-    heads = decay_s.shape[1]
-    width = values_s.shape[1] // heads
-    states = in_s.shape[1]
-    blocks = (
-        values_s.reshape(count, L, -1),
-        in_s.reshape(count, L, -1),
-        out_s.reshape(count, L, -1),
-        step_s.reshape(count, L, heads),
-        decay_s.reshape(count, L, heads),
-    )
-
-    def advance(carry, block):
-        state, total = carry
-        values_blk, in_blk, out_blk, step_blk, decay_blk = block
-        local_out, running, block_state = block_terms(
-            values_blk, in_blk, out_blk, step_blk, decay_blk, skip_gain
-        )
-        new_state = jnp.exp(running[-1])[:, None, None] * state + block_state
-        return ((new_state, total + running[-1]), (local_out, running, state, total))
-
-    initial = (jnp.zeros((heads, width, states), jnp.float32), jnp.zeros((heads,), jnp.float32))
-    return lax.scan(advance, initial, blocks)
-
-
-def link(earlier, later):
-    decay_early, state_early = earlier
-    decay_late, state_late = later
-    return (decay_early * decay_late, decay_late[:, :, None, None] * state_early + state_late)
-
-
-def group_norm(gated, norm_gain):
-    width = GROUP_HEADS * P_SIZE
-    grouped = gated.reshape(gated.shape[0], -1, width)
-    mean_square = jnp.mean(grouped * grouped, axis=-1, keepdims=True)
-    rescaled = grouped * lax.rsqrt(mean_square + EPSILON)
-    return (rescaled.reshape(gated.shape) * norm_gain).astype(jnp.bfloat16)
 
 
 def shards(
@@ -411,36 +604,67 @@
     out_weight,
     prompt_state,
 ):
-    prompt = lax.all_gather(prompt_state.astype(jnp.bfloat16), SAMPLE, axis=2, tiled=True).astype(
-        prompt_state.dtype
+    vmem = pl.BlockSpec(memory_space=pltpu.VMEM)
+    hbm = pl.BlockSpec(memory_space=pl.ANY)
+    out = pl.pallas_call(
+        kernel,
+        name="layer",
+        out_shape=jax.ShapeDtypeStruct((512, 2048), BF16),
+        in_specs=[hbm] * 4 + [vmem] * 6,
+        out_specs=vmem,
+        scratch_shapes=[
+            pltpu.VMEM((16, 16, 128, 256), BF16),
+            pltpu.VMEM((2, NZ, 512, 256), BF16),
+            pltpu.VMEM((NZ, 512, 256), BF16),
+            pltpu.VMEM((512, 2048), BF16),
+            pltpu.VMEM((512, 2048), BF16),
+            pltpu.VMEM((512, 2048), BF16),
+            pltpu.VMEM((512, 2048), F32),
+            pltpu.VMEM((512, 2048), F32),
+            pltpu.VMEM((512, 2048), BF16),
+            pltpu.VMEM((128, 2048), F32),
+            pltpu.VMEM((2, L, L), F32),
+            pltpu.VMEM((512, 32), F32),
+            pltpu.VMEM((2, 32, L), F32),
+            pltpu.VMEM((32, 2048), BF16),
+            pltpu.VMEM((128, 512), BF16),
+            pltpu.VMEM((8, 32), F32),
+            pltpu.VMEM((8, 2048), F32),
+            pltpu.VMEM((NZ, 16, 2048), BF16),
+            pltpu.VMEM((NZ, 16, 2048), BF16),
+            pltpu.VMEM((1, 1, 2048), F32),
+            pltpu.VMEM((NZ, 1, 2048), F32),
+            pltpu.VMEM((16, 2048), BF16),
+            pltpu.VMEM((16, 2048), BF16),
+            pltpu.VMEM((NZ, 16, 2048), BF16),
+            pltpu.VMEM((NZ, 16, 2048), BF16),
+            pltpu.VMEM((2048, 16), F32),
+            pltpu.SemaphoreType.DMA((3,)),
+            *GATHER_SEMS,
+            *SCAN_SEMS,
+            pltpu.SemaphoreType.DMA((NZ,)),
+            pltpu.SemaphoreType.DMA((NZ,)),
+        ],
+        compiler_params=pltpu.CompilerParams(
+            collective_id=0, has_side_effects=True, vmem_limit_bytes=56 << 20
+        ),
+    )(
+        out_weight.reshape(16, 128, 256),
+        values[0],
+        gate_values[0],
+        prompt_state.reshape(2048, 16),
+        state_in[0],
+        state_out[0],
+        step_size[0],
+        log_decay[0],
+        skip_gain.reshape(1, 32),
+        norm_gain.reshape(1, 2048),
     )
-    sweep_sample = partial(local_sweep, skip_gain=skip_gain)
-    (last_state, last_total), (local_out, running, before, totals) = jax.vmap(sweep_sample)(
-        values, state_in, state_out, step_size, log_decay
-    )
-    identity = (jnp.ones_like(last_total), jnp.zeros_like(last_state))
-    lead_decay, lead_state = entering((jnp.exp(last_total), last_state), SEQ, link, identity)
-    entry = lead_state + lead_decay[:, :, None, None] * prompt[None]
-    start = before + jnp.exp(totals)[:, :, :, None, None] * entry[:, None]
-    start_low = start.astype(jnp.bfloat16)
-    samples, tokens = (values.shape[0], values.shape[1])
-    count = tokens // L
-    out_blocks = state_out.reshape(samples, count, L, -1)
-    carried = jnp.exp(running)[..., None] * jnp.einsum(
-        "sktn,skhpn->skthp", out_blocks, start_low, preferred_element_type=jnp.float32
-    )
-    outputs = (local_out + carried).reshape(samples * tokens, -1)
-    gated = outputs * jax.nn.silu(gate_values.reshape(samples * tokens, -1).astype(jnp.float32))
-    normed = group_norm(gated, norm_gain)
-    mine = project(normed, out_weight)
-    return mine.reshape(samples, tokens, -1)
+    return out[None]
 
 
 def solution(mesh):
-    split = Mesh(
-        mesh.devices.reshape(2, 4, 2, 8, 2),
-        ("ylo", "x", "yhi", "z", "head"),
-    )
+    split = Mesh(mesh.devices.reshape(2, 4, 2, NZ, 2), ("ylo", "x", "yhi", "z", "head"))
     return jax.shard_map(
         shards,
         mesh=split,

time: 282 us -> 127 us (0.45)
  blocking collectives: 47.3 us -> 0 us
  local copies, waits for them, and re-layouts: 55 us -> 8.81 us
  waiting for transfers between devices: 27.1 us -> 0 us
  other arithmetic: 21.6 us -> 0 us
  Pallas kernels: 102 us -> 118 us
  matrix products: 14.8 us -> 0 us
  between operations: 13.6 us -> 0.01 us
    all_gather x3 -> x0, blocking collectives: 47.3 us -> none  [the longest x1 26.6 us: shards(): lax.all_gather(prompt_state.astype(jnp.bfloat16), SAMPLE, axis=2, tiled=T...]
    all_gather x2 -> x0, waiting for transfers between devices: 27 us -> none  [entering(): lax.all_gather(part.astype(kind), axis)]
    reshape x3 -> x0, local copies, waits for them, and re-layouts: 18 us -> none  [the longest x2 17.1 us: shards(): outputs = (local_out + carried).reshape(samples * tokens, -1)]
    pallas_call x1, Pallas kernels: 102 us -> 118 us  [shards(): pl.pallas_call(kernel, name='layer', out_shape=jax.ShapeDtypeStruct((512,...]
    convert_element_type x2 -> x0, local copies, waits for them, and re-layouts: 15.3 us -> none  [shards(): gate_values.reshape(samples * tokens, -1).astype(jnp.float32)]
    dot_general x9 -> x0, matrix products: 14.8 us -> none  [the longest x1 4.99 us: shards(): jnp.einsum('sktn,skhpn->skthp', out_blocks, start_low, preferred_element_...]
    convert_element_type x11 -> x0, other arithmetic: 13.8 us -> none  [the longest x1 5.13 us: group_norm(): return (rescaled.reshape(gated.shape) * norm_gain).astype(jnp.bfloat16)]
    dynamic_slice x8 -> x0, local copies, waits for them, and re-layouts: 5.24 us -> none  [local_sweep(): return lax.scan(advance, initial, blocks)]
  transfers between devices with their start and end apart: 2 -> 0, of which waited for: 2 -> 0; matrix products, arithmetic and copies ran while one was open for 6% -> 0% of each run, Pallas kernels for 0% -> 0%
where the time goes in v2:
time: 127 us
  Pallas kernels  118 us (93%)
  local copies, waits for them, and re-layouts  8.81 us (7%)
    pallas_call x1, Pallas kernels, shards(): pl.pallas_call(kernel, name='layer', out_shape=jax.ShapeDtypeStruct((512,...  118 us
    unnamed x4, local copies, waits for them, and re-layouts  8.81 us

profile of v2, /device:TPU:1, one launch (start us, length us, event | category | flops | bytes accessed | tf_op | source)
XLA Modules:
  0.0 126.9 jit_solution(14166042292061643978)
XLA Ops:
  0.0 1.7 %copy.12 = f32[1,512,32]{2,1,0:T(8,128)} copy(f32[1,512,32]{1,2,0:T(8,128)} %param.14) | data formatting | bytes 131072 | tf_op args[4]
  1.7 1.7 %copy.13 = f32[1,512,32]{2,1,0:T(8,128)} copy(f32[1,512,32]{1,2,0:T(8,128)} %param.15) | data formatting | bytes 131072 | tf_op args[5]
  3.4 2.3 %copy.11 = f32[32,64,16]{2,1,0:T(8,128)} copy(f32[32,64,16]{1,2,0:T(8,128)} %param.19) | data formatting | bytes 262144 | tf_op args[9]
  5.6 118.1 %layer.1 = bf16[512,2048]{1,0:T(8,128)(2,1)} custom-call(bf16[16,128,256]{2,1,0:T(8,128)(2,1)} %bitcast.17, bf16[512,2048]{1,0:T(8,128)(2,1)} %bitcast.13, bf16[512,2048]{1,0:T(8,128)(2,1)} %bitcast.14, f32[2048,16]{1,0:T(8,128)} %bitcast.12, bf16[512,128]{1,0:T(8,128)(2,1)} %bitcast.18, bf16[512,128]{1,0:T(8,128)(2,1)} %bitcast.19, f32[512,32]{1,0:T(8,128)} %bitcast.15, ...), custom_call_target="tpu_custom_call" | custom-call | tf_op jit(solution)/shard_map/layer/pallas_call | solution.py:609
  123.8 3.2 %copy.15 = bf16[1,512,2048]{2,1,0:T(8,128)(2,1)} copy(bf16[1,512,2048]{2,1,0:T(8,128)(2,1)} %bitcast.11) | data formatting | bytes 4194304

commit v3 on v2

--- a/solution.py
+++ b/solution.py
@@ -31,6 +31,7 @@
         "+z": {"z": lax.rem(at["z"] + 1, NZ)},
         "-z": {"z": lax.rem(at["z"] + NZ - 1, NZ)},
         "across": {"yhi": 1 - at["yhi"], "ylo": 1 - at["ylo"]},
+        "beside": {"ylo": 1 - at["ylo"]},
         "sibling": {"head": 1 - at["head"]},
     }
     return at, near
@@ -82,22 +83,30 @@
         return pltpu.make_async_copy(self.own, self.wbuf.at[self.s_own], self.ls)
 
     def give(self):
-        start = self.px * 8
-        src = self.own.at[pl.ds(start, 8)]
-        return self.copy(src, self.s_own, start, 8, self.zs.at[0], self.zr.at[self.s_own], "across")
+        src = self.own.at[pl.ds(self.byy * 4, 4)]
+        to = self.zr.at[self.s_own]
+        return self.copy(src, self.s_own, self.byy * 4, 4, self.zs.at[0], to, "across")
 
     def given(self):
-        start = self.px * 8
-        return self.copy(None, self.s_across, start, 8, self.zs.at[0], self.zr.at[self.s_across], "across")
+        to = self.zr.at[self.s_across]
+        return self.copy(None, self.s_across, self.mine * 4, 4, self.zs.at[0], to, "across")
+
+    def lend(self):
+        to = self.fr.at[self.s_across, 2]
+        return self.copy(None, self.s_across, self.mine * 4, 4, self.zs.at[15], to, "beside")
+
+    def lent(self):
+        to = self.fr.at[self.s_across, 2]
+        return self.copy(None, self.s_across, self.byy * 4, 4, self.zs.at[15], to, "beside")
 
     def give_on(self, d):
-        start = self.px * 8 + 4 * d
+        start = (self.mine if d == 0 else self.byy) * 4
         return self.copy(
             None, self.s_across, start, 4, self.fs.at[0, d], self.fr.at[self.s_across, d], WAYS[d]
         )
 
     def given_on(self, d):
-        start = (1 - self.px) * 8 + 4 * d
+        start = (self.byx if d == 0 else 3 - self.mine) * 4
         return self.copy(
             None, self.s_across, start, 4, self.fs.at[0, d], self.fr.at[self.s_across, d], WAYS[d]
         )
@@ -130,7 +139,7 @@
             c.start()
             self.sent.append(c)
         self.local().start()
-        self.slots = {"z": 3, "f": 1, "g": 0}
+        self.slots = {"z": 5, "f": 1, "g": 0}
 
     def begin_across(self):
         self.given().wait_recv()
@@ -138,11 +147,16 @@
             self.ring(self.s_across, "+z", 3),
             self.ring(self.s_across, "-z", 4),
             self.give_on(0),
-            self.give_on(1),
+            self.lend(),
         ):
             c.start()
             self.sent.append(c)
-        self.slots["z"] = 5
+
+    def go_on_across(self):
+        self.lent().wait_recv()
+        c = self.give_on(1)
+        c.start()
+        self.sent.append(c)
 
     def forward(self, n):
         fam, found = self.events(n)
@@ -249,11 +263,14 @@
 
 
 F32, BF16 = jnp.float32, jnp.bfloat16
-NT = (((1,), (1,)), ((), ()))
 
 
 def mm(a, b):
     return jnp.dot(a, b, preferred_element_type=F32)
+
+
+def nt(a, b):
+    return lax.dot_general(a, b, (((1,), (1,)), ((), ())), preferred_element_type=F32)
 
 
 def three(v):
@@ -335,11 +352,10 @@
             load = pltpu.make_async_copy(prompt_hbm, prompt_vmem, sem)
             load.start()
             load.wait()
-            eye = (iota((16, 16), 0) == iota((16, 16), 1)).astype(F32).astype(BF16)
-            low = prompt_vmem[...].astype(BF16)
-            turned = lax.dot_general(eye, low, NT, preferred_element_type=F32).astype(BF16)
-            self.tsend[...] = turned
-            self.init[...] = turned
+            for j in range(0, 32, 2):
+                two = jnp.concatenate([prompt_vmem[j], prompt_vmem[j + 1]], axis=1).astype(BF16)
+                self.tsend[:, j * P_SIZE : (j + 2) * P_SIZE] = two
+                self.init[:, j * P_SIZE : (j + 2) * P_SIZE] = two
             for k in range(1, 8):
                 self.prompt(k).start()
 
@@ -407,15 +423,18 @@
     def prepare(self):
         self.e[...] = (iota((32, 2048), 0) == lax.shift_right_logical(iota((32, 2048), 1), 6)).astype(F32).astype(BF16)
         tri = (iota((L, L), 0) >= iota((L, L), 1)).astype(F32).astype(BF16)
-        eye = (iota((32, 32), 0) == iota((32, 32), 1)).astype(F32).astype(BF16)
+        eye = (iota((L, L), 0) == iota((L, L), 1)).astype(F32).astype(BF16)
+        small = (iota((32, 32), 0) == iota((32, 32), 1)).astype(F32).astype(BF16)
         self.bt[...] = self.b_in[...].astype(F32).T.astype(BF16)
         for b in range(2):
             rows = slice(b * L, b * L + L)
-            parts = three(self.log_decay[rows])
-            run = sum(mm(tri, part) for part in parts)
+            a, m, c = [nt(tri, part) for part in three(self.log_decay[:, rows])]
+            run = a + m + c
             self.run[rows] = run
-            turned = [lax.dot_general(eye, part, NT, preferred_element_type=F32) for part in three(run)]
-            self.runt[b] = turned[0] + turned[1] + turned[2]
+            a, m, c = [nt(small, part) for part in three(run)]
+            self.runt[b] = a + m + c
+            a, m, c = [nt(eye, part) for part in three(self.step[:, rows])]
+            self.stept[rows] = a + m + c
             self.scores[b] = mm(self.c_out[rows], self.bt[:, rows])
         ends = [self.run[L - 1 : L], self.run[2 * L - 1 : 2 * L]]
         line = iota((8, 32), 0)
@@ -441,7 +460,7 @@
                 rows = slice(b * L, b * L + L)
                 run = self.run[rows]
                 self.re[rows, cols] = by_column(run, e)
-                scaled = (self.values[rows, cols].astype(F32) * by_column(self.step[rows], e)).astype(BF16)
+                scaled = (self.values[rows, cols].astype(F32) * by_column(self.stept[rows], e)).astype(BF16)
                 self.scaled[rows, cols] = scaled
                 tail = by_column(jnp.exp(run[L - 1 : L] - run), e)
                 weighted = (scaled.astype(F32) * tail).astype(BF16)
@@ -501,17 +520,31 @@
         lax.fori_loop(lo, hi, group, 0)
 
 
+ORDER = (
+    ("s", 0, 2), ("z", 0), ("across",), ("s", 2, 4), ("send",), ("m", 0, 0, 8), ("across2",), ("m", 0, 8, 16),
+    ("z", 1), ("z", 2), ("m", 1, 0, 8), ("x", 0), ("x", 1), ("m", 1, 8, 16), ("z", 3), ("z", 4), ("scan", 0),
+    ("z", 5), ("z", 6), ("x", 2), ("x", 3), ("scan", 1), ("z", 7), ("gate",), ("entered",), ("n", 0, 0, 4),
+    ("n", 1, 0, 4), ("x", 4), ("x", 5), ("across3",), ("c", 0), ("r", 0), ("r", 1), ("c", 1), ("x", 6), ("x", 7),
+    ("r", 2), ("r", 3), ("c", 2), ("o", 0), ("o", 1), ("r", 4), ("r", 5), ("c", 3), ("o", 2), ("o", 3), ("r", 6),
+    ("r", 7), ("c", 4), ("o", 4),
+)
+
+
 def kernel(
-    own, values_hbm, gate_hbm, prompt_hbm, b_in, c_out, step, log_decay, skip_gain, norm_gain,
-    result,
-    wbuf, part, got, values, gate, scaled, re, lout, normed, bs0, scores, run, runt, e, bt,
+    own, values_hbm, gate_hbm, prompt_hbm, b_hbm, c_hbm, step_hbm, decay_hbm, skip_hbm, norm_hbm,
+    result, b_in, c_out, step, log_decay, skip_gain, norm_gain,
+    wbuf, part, got, values, gate, scaled, re, lout, bs0, scores, run, runt, stept, e, bt,
     lines, wide, sout, sin, dsend, din, init, tsend, eout, entry, prompt, load, *sems,
 ):
     at, near = place()
-    first = pltpu.make_async_copy(values_hbm, values, load.at[0])
-    second = pltpu.make_async_copy(gate_hbm, gate, load.at[1])
-    first.start()
-    second.start()
+    normed = scaled
+    pairs = (
+        (decay_hbm, log_decay), (step_hbm, step), (b_hbm, b_in), (c_hbm, c_out), (skip_hbm, skip_gain),
+        (values_hbm, values), (norm_hbm, norm_gain), (gate_hbm, gate),
+    )
+    loads = [pltpu.make_async_copy(src, dst, load.at[i]) for i, (src, dst) in enumerate(pairs)]
+    for copy in loads:
+        copy.start()
     greet(at, near)
     gather = Gather(at, near, own, wbuf, sems[:7])
     scan = Scan(at, sout, sin, dsend, din, init, tsend, eout, entry, sems[7:16])
@@ -519,7 +552,7 @@
     local = Local(
         b_in=b_in, c_out=c_out, step=step, log_decay=log_decay, skip_gain=skip_gain, norm_gain=norm_gain,
         values=values, gate=gate, scaled=scaled, re=re, lout=lout, normed=normed, bs0=bs0, scores=scores,
-        run=run, runt=runt, e=e, bt=bt, lines=lines, wide=wide, sout=sout, dsend=dsend, entry=entry,
+        run=run, runt=runt, stept=stept, e=e, bt=bt, lines=lines, wide=wide, sout=sout, dsend=dsend, entry=entry,
     )
     z = at["z"]
 
@@ -533,59 +566,31 @@
         if 0 < k < 4:
             proj.combine(lax.rem(z + NZ - k, NZ))
 
+    steps = {
+        "z": gather.forward,
+        "x": gather.spread,
+        "r": gather.arrived,
+        "s": local.states,
+        "m": local.mix,
+        "n": local.normalize,
+        "c": columns,
+        "o": combine,
+        "across": gather.begin_across,
+        "across2": gather.go_on_across,
+        "across3": gather.arrived_across,
+        "scan": scan.combine,
+        "send": scan.send_states,
+        "entered": scan.entered,
+        "gate": lambda: (loads[6].wait(), loads[7].wait()),
+    }
     gather.begin()
-    scan.send_prompt(prompt_hbm, prompt, load.at[2])
+    scan.send_prompt(prompt_hbm, prompt, load.at[8])
+    for copy in loads[:5]:
+        copy.wait()
     local.prepare()
-    first.wait()
-    local.states(0, 2)
-    gather.forward(0)
-    local.states(2, 4)
-    scan.send_states()
-    gather.begin_across()
-    local.mix(0, 0, 8)
-    gather.forward(1)
-    gather.spread(0)
-    local.mix(0, 8, 16)
-    scan.combine(0)
-    gather.forward(2)
-    gather.spread(1)
-    local.mix(1, 0, 8)
-    scan.combine(1)
-    gather.forward(3)
-    gather.spread(2)
-    local.mix(1, 8, 16)
-    second.wait()
-    scan.entered()
-    local.normalize(0, 0, 4)
-    gather.forward(4)
-    gather.spread(3)
-    local.normalize(1, 0, 4)
-    gather.arrived_across()
-    columns(0)
-    gather.arrived(0)
-    gather.arrived(1)
-    columns(1)
-    gather.forward(5)
-    gather.spread(4)
-    combine(0)
-    combine(1)
-    gather.arrived(2)
-    gather.arrived(3)
-    columns(2)
-    gather.forward(6)
-    gather.spread(5)
-    combine(2)
-    gather.forward(7)
-    gather.spread(6)
-    gather.arrived(4)
-    gather.arrived(5)
-    columns(3)
-    gather.spread(7)
-    combine(3)
-    gather.arrived(6)
-    gather.arrived(7)
-    columns(4)
-    combine(4)
+    loads[5].wait()
+    for what, *how in ORDER:
+        steps[what](*how)
     for k in range(NZ):
         proj.copy(k).wait_send()
     scan.finish()
@@ -605,14 +610,20 @@
     prompt_state,
 ):
     vmem = pl.BlockSpec(memory_space=pltpu.VMEM)
-    hbm = pl.BlockSpec(memory_space=pl.ANY)
+    hbm = pl.BlockSpec(memory_space=pltpu.HBM)
     out = pl.pallas_call(
         kernel,
         name="layer",
         out_shape=jax.ShapeDtypeStruct((512, 2048), BF16),
-        in_specs=[hbm] * 4 + [vmem] * 6,
+        in_specs=[hbm] * 10,
         out_specs=vmem,
         scratch_shapes=[
+            pltpu.VMEM((512, 128), BF16),
+            pltpu.VMEM((512, 128), BF16),
+            pltpu.VMEM((32, 512), F32),
+            pltpu.VMEM((32, 512), F32),
+            pltpu.VMEM((1, 32), F32),
+            pltpu.VMEM((1, 2048), F32),
             pltpu.VMEM((16, 16, 128, 256), BF16),
             pltpu.VMEM((2, NZ, 512, 256), BF16),
             pltpu.VMEM((NZ, 512, 256), BF16),
@@ -621,11 +632,11 @@
             pltpu.VMEM((512, 2048), BF16),
             pltpu.VMEM((512, 2048), F32),
             pltpu.VMEM((512, 2048), F32),
-            pltpu.VMEM((512, 2048), BF16),
             pltpu.VMEM((128, 2048), F32),
             pltpu.VMEM((2, L, L), F32),
             pltpu.VMEM((512, 32), F32),
             pltpu.VMEM((2, 32, L), F32),
+            pltpu.VMEM((512, 32), F32),
             pltpu.VMEM((32, 2048), BF16),
             pltpu.VMEM((128, 512), BF16),
             pltpu.VMEM((8, 32), F32),
@@ -638,27 +649,32 @@
             pltpu.VMEM((16, 2048), BF16),
             pltpu.VMEM((NZ, 16, 2048), BF16),
             pltpu.VMEM((NZ, 16, 2048), BF16),
-            pltpu.VMEM((2048, 16), F32),
-            pltpu.SemaphoreType.DMA((3,)),
+            pltpu.VMEM((32, 16, P_SIZE), F32),
+            pltpu.SemaphoreType.DMA((9,)),
             *GATHER_SEMS,
             *SCAN_SEMS,
             pltpu.SemaphoreType.DMA((NZ,)),
             pltpu.SemaphoreType.DMA((NZ,)),
         ],
         compiler_params=pltpu.CompilerParams(
-            collective_id=0, has_side_effects=True, vmem_limit_bytes=56 << 20
+            collective_id=0, has_side_effects=True, vmem_limit_bytes=46 << 20
         ),
     )(
-        out_weight.reshape(16, 128, 256),
-        values[0],
-        gate_values[0],
-        prompt_state.reshape(2048, 16),
-        state_in[0],
-        state_out[0],
-        step_size[0],
-        log_decay[0],
-        skip_gain.reshape(1, 32),
-        norm_gain.reshape(1, 2048),
+        *[
+            pltpu.with_memory_space_constraint(operand, pltpu.HBM)
+            for operand in (
+                out_weight.reshape(16, 128, 256),
+                values[0],
+                gate_values[0],
+                prompt_state.transpose(0, 2, 1),
+                state_in[0],
+                state_out[0],
+                step_size[0].T,
+                log_decay[0].T,
+                skip_gain.reshape(1, 32),
+                norm_gain.reshape(1, 2048),
+            )
+        ]
     )
     return out[None]
 

time: 127 us -> 102 us (0.80)
  Pallas kernels: 118 us -> 101 us
  local copies, waits for them, and re-layouts: 8.81 us -> 1.32 us
    pallas_call x1, Pallas kernels: 118 us -> 101 us  [shards(): pl.pallas_call(kernel, name='layer', out_shape=jax.ShapeDtypeStruct((512,...]
    unnamed x4 -> x1, local copies, waits for them, and re-layouts: 8.81 us -> 1.32 us
where the time goes in v3:
time: 102 us
  Pallas kernels  101 us (99%)
  local copies, waits for them, and re-layouts  1.32 us (1%)
    pallas_call x1, Pallas kernels, shards(): pl.pallas_call(kernel, name='layer', out_shape=jax.ShapeDtypeStruct((512,...  101 us

profile of v3, /device:TPU:1, one launch (start us, length us, event | category | flops | bytes accessed | tf_op | source)
XLA Modules:
  0.0 102.3 jit_solution(14412704444838792257)
XLA Ops:
  0.0 101.0 %layer.1 = bf16[512,2048]{1,0:T(8,128)(2,1)S(1)} custom-call(bf16[16,128,256]{2,1,0:T(8,128)(2,1)} %bitcast.18, bf16[512,2048]{1,0:T(8,128)(2,1)} %bitcast.16, bf16[512,2048]{1,0:T(8,128)(2,1)} %bitcast.17, f32[32,16,64]{2,1,0:T(8,128)} %bitcast.19, bf16[512,128]{1,0:T(8,128)(2,1)} %bitcast.20, bf16[512,128]{1,0:T(8,128)(2,1)} %bitcast.21, ...), custom_call_target="tpu_custom_call" | custom-call | tf_op jit(solution)/shard_map/layer/pallas_call | solution.py:614
  101.0 1.3 %copy.12 = bf16[1,512,2048]{2,1,0:T(8,128)(2,1)} copy(bf16[1,512,2048]{2,1,0:T(8,128)(2,1)S(1)} %bitcast.15) | data formatting | bytes 4194304

commit v4 on v3

--- a/solution.py
+++ b/solution.py
@@ -76,28 +76,32 @@
             found.append((self.shard(fam, self.at["z"] + 1 + k), k, "-z"))
         return fam, found
 
-    def ring(self, s, way, slot, src=None):
-        return self.copy(src, s, self.mine * 4, 4, self.zs.at[slot], self.zr.at[s], way)
+    def ring(self, s, way, half, slot, own=False):
+        start = self.mine * 4 + 2 * half
+        src = self.own.at[pl.ds(start, 2)] if own else None
+        return self.copy(src, s, start, 2, self.zs.at[slot, half], self.zr.at[s, half], way)
 
     def local(self):
         return pltpu.make_async_copy(self.own, self.wbuf.at[self.s_own], self.ls)
 
-    def give(self):
-        src = self.own.at[pl.ds(self.byy * 4, 4)]
-        to = self.zr.at[self.s_own]
-        return self.copy(src, self.s_own, self.byy * 4, 4, self.zs.at[0], to, "across")
-
-    def given(self):
-        to = self.zr.at[self.s_across]
-        return self.copy(None, self.s_across, self.mine * 4, 4, self.zs.at[0], to, "across")
+    def give(self, half):
+        start = self.byy * 4 + 2 * half
+        src = self.own.at[pl.ds(start, 2)]
+        to = self.zr.at[self.s_own, half]
+        return self.copy(src, self.s_own, start, 2, self.zs.at[0, half], to, "across")
+
+    def given(self, half):
+        to = self.zr.at[self.s_across, half]
+        start = self.mine * 4 + 2 * half
+        return self.copy(None, self.s_across, start, 2, self.zs.at[0, half], to, "across")
 
     def lend(self):
         to = self.fr.at[self.s_across, 2]
-        return self.copy(None, self.s_across, self.mine * 4, 4, self.zs.at[15], to, "beside")
+        return self.copy(None, self.s_across, self.mine * 4, 4, self.zs.at[16, 0], to, "beside")
 
     def lent(self):
         to = self.fr.at[self.s_across, 2]
-        return self.copy(None, self.s_across, self.byy * 4, 4, self.zs.at[15], to, "beside")
+        return self.copy(None, self.s_across, self.byy * 4, 4, self.zs.at[16, 0], to, "beside")
 
     def give_on(self, d):
         start = (self.mine if d == 0 else self.byy) * 4
@@ -128,29 +132,30 @@
         start = far * 4 + (0, 2, 1, 3)[d]
         return self.copy(None, s, start, 1, self.gs.at[0, d], self.gr.at[s, d], WAYS[d])
 
-    def begin(self):
-        src = self.own.at[pl.ds(self.mine * 4, 4)]
-        self.sent = []
-        for c in (
-            self.ring(self.s_own, "+z", 1, src),
-            self.ring(self.s_own, "-z", 2, src),
-            self.give(),
-        ):
+    def send(self, *copies):
+        for c in copies:
             c.start()
             self.sent.append(c)
+
+    def begin(self):
+        self.sent = []
+        for i in range(2):
+            self.send(
+                self.ring(self.s_own, "+z", i, 1, True),
+                self.ring(self.s_own, "-z", 1 - i, 2, True),
+                self.give(i),
+            )
         self.local().start()
         self.slots = {"z": 5, "f": 1, "g": 0}
 
     def begin_across(self):
-        self.given().wait_recv()
-        for c in (
-            self.ring(self.s_across, "+z", 3),
-            self.ring(self.s_across, "-z", 4),
-            self.give_on(0),
-            self.lend(),
-        ):
-            c.start()
-            self.sent.append(c)
+        for i in range(2):
+            self.given(i).wait_recv()
+            self.send(
+                self.ring(self.s_across, "+z", i, 3),
+                self.ring(self.s_across, "-z", i, 4),
+            )
+        self.send(self.give_on(0), self.lend())
 
     def go_on_across(self):
         self.lent().wait_recv()
@@ -160,19 +165,20 @@
 
     def forward(self, n):
         fam, found = self.events(n)
+        slots = [(self.slots["z"] + i, self.slots["f"] + i) for i in range(len(found))]
+        self.slots["f"] += len(found)
+        for i in range(2):
+            for (s, k, way), (zslot, fslot) in zip(found, slots):
+                half = i if way == "+z" or fam == 1 else 1 - i
+                self.ring(s, way, half, 0).wait_recv()
+                last = k + 1 == (4 if (fam == 0) == (way == "+z") else 3)
+                if not last:
+                    self.send(self.ring(s, way, half, zslot))
+                self.send(self.first(s, half, fslot), self.first(s, 2 + half, fslot))
         for s, k, way in found:
-            self.ring(s, way, 0).wait_recv()
-            last = k + 1 == ((4 if fam == 0 else 3) if way == "+z" else (3 if fam == 0 else 4))
+            last = k + 1 == (4 if (fam == 0) == (way == "+z") else 3)
             if not last:
-                c = self.ring(s, way, self.slots["z"])
                 self.slots["z"] += 1
-                c.start()
-                self.sent.append(c)
-            for d in range(4):
-                c = self.first(s, d, self.slots["f"])
-                c.start()
-                self.sent.append(c)
-            self.slots["f"] += 1
 
     def spread(self, n):
         fam, found = self.events(n)
@@ -220,8 +226,8 @@
 
 
 GATHER_SEMS = [
-    pltpu.SemaphoreType.DMA((17,)),
-    pltpu.SemaphoreType.DMA((16,)),
+    pltpu.SemaphoreType.DMA((17, 2)),
+    pltpu.SemaphoreType.DMA((16, 2)),
     pltpu.SemaphoreType.DMA((15, 4)),
     pltpu.SemaphoreType.DMA((16, 4)),
     pltpu.SemaphoreType.DMA((14, 4)),
@@ -281,8 +287,7 @@
 
 
 def by_column(v, e):
-    a, b, c = three(v)
-    return mm(a, e) + mm(b, e) + mm(c, e)
+    return mm(jnp.concatenate(three(v), axis=1), e)
 
 
 def iota(shape, dim):
@@ -421,7 +426,8 @@
         self.__dict__.update(refs)
 
     def prepare(self):
-        self.e[...] = (iota((32, 2048), 0) == lax.shift_right_logical(iota((32, 2048), 1), 6)).astype(F32).astype(BF16)
+        picks = iota((32, 2048), 0) == lax.shift_right_logical(iota((32, 2048), 1), 6)
+        self.e[...] = jnp.concatenate([picks.astype(F32)] * 3, axis=0).astype(BF16)
         tri = (iota((L, L), 0) >= iota((L, L), 1)).astype(F32).astype(BF16)
         eye = (iota((L, L), 0) == iota((L, L), 1)).astype(F32).astype(BF16)
         small = (iota((32, 32), 0) == iota((32, 32), 1)).astype(F32).astype(BF16)
@@ -521,12 +527,13 @@
 
 
 ORDER = (
-    ("s", 0, 2), ("z", 0), ("across",), ("s", 2, 4), ("send",), ("m", 0, 0, 8), ("across2",), ("m", 0, 8, 16),
-    ("z", 1), ("z", 2), ("m", 1, 0, 8), ("x", 0), ("x", 1), ("m", 1, 8, 16), ("z", 3), ("z", 4), ("scan", 0),
-    ("z", 5), ("z", 6), ("x", 2), ("x", 3), ("scan", 1), ("z", 7), ("gate",), ("entered",), ("n", 0, 0, 4),
-    ("n", 1, 0, 4), ("x", 4), ("x", 5), ("across3",), ("c", 0), ("r", 0), ("r", 1), ("c", 1), ("x", 6), ("x", 7),
-    ("r", 2), ("r", 3), ("c", 2), ("o", 0), ("o", 1), ("r", 4), ("r", 5), ("c", 3), ("o", 2), ("o", 3), ("r", 6),
-    ("r", 7), ("c", 4), ("o", 4),
+    ("gate",), ("s", 3, 4), ("s", 0, 1), ("across",), ("s", 1, 2), ("s", 2, 3), ("z", 0), ("z", 1),
+    ("m", 1, 12, 16), ("send",), ("z", 2), ("across2",), ("m", 1, 0, 4), ("m", 1, 8, 12), ("m", 1, 4, 8), ("z", 3),
+    ("m", 0, 12, 16), ("m", 0, 4, 8), ("x", 2), ("x", 0), ("across3",), ("x", 1), ("scan", 0), ("x", 3),
+    ("scan", 1), ("r", 0), ("m", 0, 8, 12), ("z", 4), ("z", 5), ("r", 1), ("m", 0, 0, 4), ("x", 4), ("entered",),
+    ("n", 0, 0, 4), ("r", 3), ("x", 5), ("r", 2), ("n", 1, 0, 4), ("z", 7), ("c", 1), ("z", 6), ("c", 2), ("c", 0),
+    ("x", 7), ("r", 4), ("o", 1), ("x", 6), ("r", 5), ("c", 3), ("o", 0), ("o", 2), ("r", 6), ("r", 7), ("c", 4),
+    ("o", 3), ("o", 4),
 )
 
 
@@ -637,7 +644,7 @@
             pltpu.VMEM((512, 32), F32),
             pltpu.VMEM((2, 32, L), F32),
             pltpu.VMEM((512, 32), F32),
-            pltpu.VMEM((32, 2048), BF16),
+            pltpu.VMEM((96, 2048), BF16),
             pltpu.VMEM((128, 512), BF16),
             pltpu.VMEM((8, 32), F32),
             pltpu.VMEM((8, 2048), F32),

time: 102 us -> 98.1 us (0.962)
  Pallas kernels: 101 us -> 96.7 us
    pallas_call x1, Pallas kernels: 101 us -> 96.7 us  [shards(): pl.pallas_call(kernel, name='layer', out_shape=jax.ShapeDtypeStruct((512,...]
where the time goes in v4:
time: 98.1 us; the launch traced here: 98 us
  Pallas kernels  96.7 us (99%)
  local copies, waits for them, and re-layouts  1.32 us (1%)
    pallas_call x1, Pallas kernels, shards(): pl.pallas_call(kernel, name='layer', out_shape=jax.ShapeDtypeStruct((512,...  96.7 us

profile of v4, /device:TPU:1, one launch (start us, length us, event | category | flops | bytes accessed | tf_op | source)
XLA Modules:
  0.0 98.0 jit_solution(14660611405458787755)
XLA Ops:
  0.0 96.7 %layer.1 = bf16[512,2048]{1,0:T(8,128)(2,1)S(1)} custom-call(bf16[16,128,256]{2,1,0:T(8,128)(2,1)} %bitcast.18, bf16[512,2048]{1,0:T(8,128)(2,1)} %bitcast.16, bf16[512,2048]{1,0:T(8,128)(2,1)} %bitcast.17, f32[32,16,64]{2,1,0:T(8,128)} %bitcast.19, bf16[512,128]{1,0:T(8,128)(2,1)} %bitcast.20, bf16[512,128]{1,0:T(8,128)(2,1)} %bitcast.21, ...), custom_call_target="tpu_custom_call" | custom-call | tf_op jit(solution)/shard_map/layer/pallas_call | solution.py:621
  96.7 1.3 %copy.12 = bf16[1,512,2048]{2,1,0:T(8,128)(2,1)} copy(bf16[1,512,2048]{2,1,0:T(8,128)(2,1)S(1)} %bitcast.15) | data formatting | bytes 4194304
